TPU v7x, 512 devices: a whole 4x4x16 slice. The times are simulated.
512 devices in a mesh: batch: 64 (over z_lo, y, core), space: 8 (over x, z_hi).
Axes of the slice: x: 4, y: 4, z: 16 (z_hi: 2, z_lo: 8; z = z_hi * 8 + z_lo), core: 2. Of those that a mesh axis runs over, the one named last changes fastest.
Arguments:
- acts: bfloat16 [64, 32, 64, 640], P('batch', 'space'), may hold values from -6 to 6
- conv_weight: bfloat16 [5760, 640], P('batch', 'space'), may hold values from -0.078125 to 0.078125
- conv_bias: float32 [640], replicated, may hold values from -4 to 4
- out_cotangent: bfloat16 [64, 32, 64, 640], P('batch', 'space'), may hold values from -6 to 6
- basis_in: bfloat16 [5760, 64], P('batch'), may hold values from -0.078125 to 0.078125
- basis_out: bfloat16 [640, 64], P('batch'), may hold values from -0.25 to 0.25
- query_ids: int32 [8], replicated, may hold values from 0 to 63
Outputs:
- activated: bfloat16 [64, 32, 64, 640], P('batch', 'space')
- basis_in_new: bfloat16 [5760, 64], P('batch')
- scores: float32 [8, 64], P(None, 'batch')
All inputs are finite; a program needn't handle non-finite values.
Results may differ from a plain program's by a relative error of at most 0.0031.
Values may be sent and summed in bfloat16 or wider, within the bound.
No kernel may reach another device: no remote copies, remote signals or barrier semaphores. Data moves between devices by JAX's collectives and lax.ppermute only.
A program may use at most 64 MiB of HBM per device.

v0:
```python
import math

import jax
import jax.numpy as jnp
from jax import lax
from jax.sharding import PartitionSpec as P

DAMPING = 0.1


def extended(value, sides, width):
    for axis, dim in sides:
        size, length = (lax.axis_size(axis), value.shape[dim])
        up = [(i, (i + 1) % size) for i in range(size - 1)]
        down = [(j, i) for i, j in up]
        last = lax.slice_in_dim(value, length - width, length, axis=dim)
        initial = lax.slice_in_dim(value, 0, width, axis=dim)
        before = lax.ppermute(last, axis, up)
        after = lax.ppermute(initial, axis, down)
        value = jnp.concatenate([before, value, after], axis=dim)
    return value


def add_columns(segment, operand):
    return jnp.dot(operand, segment, preferred_element_type=jnp.float32)


def add_with_norms(segment, operand):
    summed = add_columns(segment, operand)
    squares = jnp.sum(jnp.square(segment.astype(jnp.float32)), axis=0)
    return (summed, squares)


def contract_rows(left_side, right_side):
    return lax.dot_general(
        left_side, right_side, (((0,), (0,)), ((), ())), preferred_element_type=jnp.float32
    )


def per_device(acts, conv_weight, conv_bias, out_cotangent, basis_in, basis_out, query_ids):
    ex_local, band_rows, band_cols, channels = acts.shape
    padded = extended(acts, (("space", 1),), 1)
    padded = jnp.pad(padded, ((0, 0), (0, 0), (1, 1), (0, 0)))
    shifted = [
        padded[:, row_shift : row_shift + band_rows, col_shift : col_shift + band_cols, :]
        for row_shift in range(3)
        for col_shift in range(3)
    ]
    positions = ex_local * band_rows * band_cols
    patches = jnp.stack(shifted, axis=3).reshape(positions, 9 * channels)
    kernel_cols = lax.all_gather(conv_weight, "batch", axis=0, tiled=True)
    preact = jnp.dot(
        patches,
        lax.all_gather(kernel_cols, "space", axis=1, tiled=True),
        preferred_element_type=jnp.float32,
    )
    preact = preact + conv_bias
    sigmoid_pre = jax.nn.sigmoid(preact)
    activated = (preact * sigmoid_pre).astype(jnp.bfloat16).reshape(acts.shape)
    grad_pre = (
        out_cotangent.reshape(positions, channels).astype(jnp.float32)
        * sigmoid_pre
        * (1.0 + preact * (1.0 - sigmoid_pre))
    ).astype(jnp.bfloat16)
    basis_rank = basis_in.shape[1]
    probe_in = add_columns(lax.all_gather(basis_in, "batch", axis=0, tiled=True), patches).astype(
        jnp.bfloat16
    )
    probe_out = add_columns(
        lax.all_gather(basis_out, "batch", axis=0, tiled=True), grad_pre
    ).astype(jnp.bfloat16)
    term_in = contract_rows(patches, probe_in)
    term_out = contract_rows(grad_pre, probe_out)
    summed = lax.psum((term_in, term_out), "space")
    owned_in, owned_out = (
        lax.psum_scatter(summed[0], "batch", scatter_dimension=0, tiled=True),
        lax.psum_scatter(summed[1], "batch", scatter_dimension=0, tiled=True),
    )
    total_positions = positions * lax.axis_size("batch") * lax.axis_size("space")
    basis_in_new = (owned_in / total_positions).astype(jnp.bfloat16)
    basis_out_new = (owned_out / total_positions).astype(jnp.bfloat16)
    raw_in, square_in = add_with_norms(
        lax.all_gather(basis_in_new, "batch", axis=0, tiled=True), patches
    )
    raw_out, square_out = add_with_norms(
        lax.all_gather(basis_out_new, "batch", axis=0, tiled=True), grad_pre
    )
    scale_in = jnp.sqrt(square_in)
    scale_out = jnp.sqrt(square_out)
    feat_in = (
        (raw_in / scale_in)
        .astype(jnp.bfloat16)
        .reshape(ex_local, band_rows * band_cols, basis_rank)
    )
    feat_out = (
        (raw_out / scale_out)
        .astype(jnp.bfloat16)
        .reshape(ex_local, band_rows * band_cols, basis_rank)
    )
    height = band_rows * lax.axis_size("space")
    projected = (
        jnp.einsum("epi,epj->eij", feat_out, feat_in, preferred_element_type=jnp.float32) / height
    )
    projected = lax.psum(projected, "space")
    scaled = projected / (scale_out[:, None] * scale_in[None, :] + DAMPING)
    all_projs = lax.all_gather(projected, "batch", axis=0, tiled=True)
    queries = jnp.take(all_projs, query_ids, axis=0)
    scores = jnp.einsum("qij,eij->qe", queries, scaled, precision=lax.Precision.HIGHEST) / (
        basis_rank * math.sqrt(basis_rank)
    )
    return (activated, basis_in_new, scores)


def solution(mesh):
    return jax.shard_map(
        per_device,
        mesh=mesh,
        in_specs=(
            P("batch", "space", None, None),
            P("batch", "space"),
            P(),
            P("batch", "space", None, None),
            P("batch", None),
            P("batch", None),
            P(),
        ),
        out_specs=(P("batch", "space", None, None), P("batch", None), P(None, "batch")),
        check_vma=False,
    )
```

profile of v0, /device:TPU:1, one launch (start us, length us, event | category | flops | bytes accessed | tf_op | source)
XLA Modules:
  0.0 1847.2 jit_solution(3337683036946885710)
XLA Ops:
  7.2 132.7 %all-gather = bf16[64,90,80]{1,2,0:T(8,128)(2,1)S(1)} all-gather(bf16[1,90,80]{1,2,0:T(8,128)(2,1)} %bitcast.90), channel_id=1, replica_groups=mesh['batch'=64,'space'=8] {'batch'}, dimensions={0}, use_global_device_ids=true | all-gather | bytes 936000 | tf_op jit(solution)/shard_map/all_gather | solution.py:51
  140.3 2.8 reshape.103
  143.2 8.0 collective-permute-start
  151.2 1.3 collective-permute-start.1
  152.5 167.6 %all-gather.1 = bf16[64,90,64]{1,2,0:T(8,128)(2,1)S(1)} all-gather(bf16[1,90,64]{1,2,0:T(8,128)(2,1)S(1)} %bitcast.91), channel_id=1, replica_groups=mesh['batch'=64,'space'=8] {'batch'}, dimensions={0}, use_global_device_ids=true | all-gather | bytes 748800 | tf_op jit(solution)/shard_map/all_gather | solution.py:66
  320.1 165.3 %all-gather.2 = bf16[64,10,64]{2,1,0:T(8,128)(2,1)S(1)} all-gather(bf16[1,10,64]{2,1,0:T(8,128)(2,1)S(1)} %bitcast.92), channel_id=1, replica_groups=mesh['batch'=64,'space'=8] {'batch'}, dimensions={0}, use_global_device_ids=true | all-gather | bytes 83200 | tf_op jit(solution)/shard_map/all_gather | solution.py:70
  486.2 2.4 reshape.105
  489.4 0.9 fusion.25
  490.9 2.0 copy.14
  492.9 0.9 copy.22
  493.7 4.5 fusion.3
  498.3 6.4 fusion.11
  504.7 1.3 fusion.2
  506.1 1.3 dynamic-slice
  508.6 821.8 %all-reduce.7.cloned.1.call-done = (f32[5760,64]{0,1:T(8,128)}, f32[640,64]{1,0:T(8,128)}) async-done(((f32[5760,64]{0,1:T(8,128)}, f32[640,64]{1,0:T(8,128)}), (f32[5760,64]{0,1:T(8,128)}, f32[640,64]{1,0:T(8,128)})) %all-reduce.7.cloned.1.call-update) | async-done | bytes 1638416
  1330.4 0.9 constant_dynamic-slice_fusion.1
  1331.3 0.7 constant_dynamic-slice_fusion
  1332.0 66.9 %all-reduce.4 = (f32[90,64]{0,1:T(8,128)S(1)}, f32[10,64]{1,0:T(8,128)S(1)}) all-reduce(f32[90,64]{0,1:T(8,128)S(1)} %constant_dynamic-slice_fusion.1, f32[10,64]{1,0:T(8,128)S(1)} %constant_dynamic-slice_fusion), channel_id=1, replica_groups=mesh['batch'=64,'space'=8] {'space'}, use_global_device_ids=true, to_apply=%region_0.1 | all-reduce | flops 6400 | bytes 51200 | tf_op jit(solution)/shard_map/psum | solution.py:74
  1398.9 130.7 %all-gather.4 = bf16[64,90,64]{1,2,0:T(8,128)(2,1)S(1)} all-gather(bf16[1,90,64]{1,2,0:T(8,128)(2,1)S(1)} %fusion.45), channel_id=1, replica_groups=mesh['batch'=64,'space'=8] {'batch'}, dimensions={0}, use_global_device_ids=true | all-gather | bytes 748800 | tf_op jit(solution)/shard_map/all_gather | solution.py:83
  1529.6 1.6 copy.17
  1531.2 3.1 reshape.111
  1534.4 1.4 multiply_reduce_fusion
  1535.8 114.8 %all-gather.3 = bf16[64,10,64]{2,1,0:T(8,128)(2,1)S(1)} all-gather(bf16[1,10,64]{2,1,0:T(8,128)(2,1)S(1)} %fusion.29), channel_id=1, replica_groups=mesh['batch'=64,'space'=8] {'batch'}, dimensions={0}, use_global_device_ids=true | all-gather | bytes 83200 | tf_op jit(solution)/shard_map/all_gather | solution.py:86
  1650.5 0.7 reshape.109
  1651.3 1.0 multiply_reduce_fusion.1
  1652.3 1.2 fusion.1
  1653.5 2.3 fusion.6
  1655.7 60.8 %psum.23 = f32[1,64,64]{2,1,0:T(8,128)} all-reduce(f32[1,64,64]{2,1,0:T(8,128)S(1)} %fusion.6), channel_id=1, replica_groups=mesh['batch'=64,'space'=8] {'space'}, use_global_device_ids=true, to_apply=%region_6.7 | all-reduce | flops 4096 | bytes 32768 | tf_op jit(solution)/shard_map/psum | solution.py:104
  1717.2 0.8 add_divide_fusion.1
  1718.1 119.1 %all-gather.10.cloned.1.call-done = f32[64,64,64]{2,1,0:T(8,128)} async-done(((f32[1,64,64]{2,1,0:T(8,128)}), f32[64,64,64]{2,1,0:T(8,128)}) %all-gather.10.cloned.1.call-update) | async-done | bytes 1048592 | tf_op jit(solution)/shard_map/all_gather | solution.py:106
  1837.2 2.2 gather_fusion
  1839.5 1.2 fusion.8
  (47 shorter events, 3.4 us)
Async XLA Ops:
  7.2 491.1 %all-gather.8.cloned.1.call-start = ((), (), s32[]{:S(2)}) async-start(), calls=%async_computation | async-start | bytes 8294400 | tf_op jit(solution)/shard_map/all_gather | solution.py:54
  139.9 3.2 copy-start
  139.9 12.6 copy-start.4
  140.0 180.1 %copy-start.5 = (bf16[10,64]{1,0:T(8,128)(2,1)S(1)}, bf16[10,64]{1,0:T(8,128)(2,1)}, u32[]{:S(2)}) copy-start(bf16[10,64]{1,0:T(8,128)(2,1)} %param.12) | copy-start | bytes 3844
  143.1 1187.3 %all-reduce.7.cloned.1.call-start = ((), (), s32[]{:S(2)}) async-start(), calls=%async_computation.2 | async-start | bytes 3604480
  143.2 345.4 %collective-permute-start = (bf16[1,1,64,640]{3,2,1,0:T(8,128)(2,1)S(1)}, bf16[1,1,64,640]{3,2,1,0:T(8,128)(2,1)S(1)}, u32[]{:S(2)}, u32[]{:S(2)}) collective-permute-start(bf16[1,1,64,640]{3,2,1,0:T(8,128)(2,1)S(1)} %get-tuple-element.9), channel_id=1, source_target_pairs={{0,1},{1,2},{2,3},{3,4},{4,5},{5,6},{6,7},{8,9},{9,10},{10,11},{11... | collective-permute-start | bytes 245768 | tf_op jit(solution)/shard_map/ppermute | solution.py:18
  151.2 337.4 %collective-permute-start.1 = (bf16[1,1,64,640]{3,2,1,0:T(8,128)(2,1)S(1)}, bf16[1,1,64,640]{3,2,1,0:T(8,128)(2,1)S(1)}, u32[]{:S(2)}, u32[]{:S(2)}) collective-permute-start(bf16[1,1,64,640]{3,2,1,0:T(8,128)(2,1)S(1)} %get-tuple-element.10), channel_id=1, source_target_pairs={{1,0},{2,1},{3,2},{4,3},{5,4},{6,5},{7,6},{9,8},{10,9},{11,10},{12... | collective-permute-start | bytes 245768 | tf_op jit(solution)/shard_map/ppermute | solution.py:19
  488.6 0.6 copy-start.1
  493.7 4.6 copy-start.6
  506.0 1331.2 %all-gather.10.cloned.1.call-start = ((), (), s32[]{:S(2)}) async-start(), calls=%async_computation.1 | async-start | bytes 2129920 | tf_op jit(solution)/shard_map/all_gather | solution.py:106
  1398.9 136.8 %copy-start.2 = (f32[90,64]{0,1:T(8,128)}, f32[90,64]{0,1:T(8,128)S(1)}, u32[]{:S(2)}) copy-start(f32[90,64]{0,1:T(8,128)S(1)} %get-tuple-element.5) | copy-start | bytes 69124
  1534.4 182.2 %copy-start.7 = (s32[8]{0:T(128)S(1)}, s32[8]{0:T(128)}, u32[]{:S(2)}) copy-start(s32[8]{0:T(128)} %param.13) | copy-start | bytes 100
  1651.3 65.3 %copy-start.3 = (f32[90,64]{0,1:T(8,128)S(1)}, f32[90,64]{0,1:T(8,128)}, u32[]{:S(2)}) copy-start(f32[90,64]{0,1:T(8,128)} %copy-done.2) | copy-start | bytes 69124
Sparse Core Ops, SparseCore 0:
  143.2 265.6 all-gather.7
  506.1 824.2 all-reduce.6
  1716.7 120.4 all-gather.9
where the time goes:
time: 1850 us
  waiting for transfers between devices  941 us (51%)
  blocking collectives  839 us (45%)
  local copies, waits for them, and re-layouts  20.8 us (1%)
    unnamed x4, waiting for transfers between devices  822 us
    all_gather x1, blocking collectives, per_device(): lax.all_gather(basis_in, 'batch', axis=0, tiled=True)  168 us
    all_gather x1, blocking collectives, per_device(): lax.all_gather(basis_out, 'batch', axis=0, tiled=True)  165 us
    all_gather x1, blocking collectives, per_device(): kernel_cols = lax.all_gather(conv_weight, 'batch', axis=0, tiled=True)  133 us
    all_gather x1, blocking collectives, per_device(): lax.all_gather(basis_in_new, 'batch', axis=0, tiled=True)  131 us
    all_gather x1, waiting for transfers between devices, per_device(): all_projs = lax.all_gather(projected, 'batch', axis=0, tiled=True)  119 us
    all_gather x1, blocking collectives, per_device(): lax.all_gather(basis_out_new, 'batch', axis=0, tiled=True)  115 us
    psum x1, blocking collectives, per_device(): summed = lax.psum((term_in, term_out), 'space')  66.9 us
  transfers between devices with their start and end apart: 5, of which 2 were waited for; matrix products, arithmetic and copies ran while one was open for 1% of the time, Pallas kernels for 0%

commit v1 on v0

v1 whole, which is shorter than its diff:
```python
import math

import jax
import jax.numpy as jnp
from jax import lax
from jax.sharding import Mesh
from jax.sharding import PartitionSpec as P

DAMPING = 0.1
SPLIT = (("zl", 8), ("y", 4), ("c", 2), ("x", 4), ("zh", 2))
AXES = tuple(name for name, _ in SPLIT)
SIZES = dict(SPLIT)
BATCH = ("zl", "y", "c")
SPACE = ("x", "zh")
Z = ("zh", "zl")
F32, BF16 = jnp.float32, jnp.bfloat16

CH, RANK, TAPS = 640, 64, 9
PATCH = TAPS * CH
ROWS = PATCH // 64
COLS = CH // 8
WIDE = 768
SLOT = WIDE + 128


def exchange(value, axes):
    return lax.all_to_all(value, axes, 0, 0, tiled=True)


def gather(value, axes):
    count = math.prod(SIZES[a] for a in axes)
    copies = jnp.broadcast_to(value[None], (count,) + value.shape)
    return exchange(lax.optimization_barrier(copies), axes)


def halo(value):
    up = [(i, i + 1) for i in range(7)]
    down = [(j, i) for i, j in up]
    before = lax.ppermute(value[-1:], SPACE, up)
    after = lax.ppermute(value[:1], SPACE, down)
    return jnp.concatenate([before, value, after], axis=0)


def gather_weights(conv_weight, basis_in, basis_out):
    at = lax.axis_index(SPACE) * 8
    kernel = conv_weight.T
    basis = lax.dynamic_slice_in_dim(basis_in.T, at, 8, axis=0)
    outer = lax.dynamic_slice_in_dim(basis_out.T, at, 8, axis=0)
    rows = jnp.pad(jnp.concatenate([kernel, basis], axis=0), ((0, 0), (0, 128 - ROWS)))
    rows = lax.dynamic_update_slice(rows, outer, (COLS, ROWS))
    got = gather(rows, Z).reshape(2, 8, COLS + 8, 128)

    def merged(part, width):
        flat = part.transpose(0, 2, 1, 3).reshape(part.shape[0] * part.shape[2], -1)
        return jnp.pad(flat, ((0, 0), (0, WIDE - flat.shape[1])))

    joined = jnp.concatenate(
        [
            merged(got[:, :, :COLS, :ROWS], ROWS),
            merged(got[:, :, COLS:, :ROWS], ROWS),
            merged(got[:, :, COLS:, ROWS : ROWS + 10], 10),
        ],
        axis=0,
    )
    plane = gather(joined, ("y", "x"))
    both = gather(plane, ("c",)).reshape(2, 4, 4, 192, WIDE)
    weight = both[:, :, :, :160].reshape(8, CH, WIDE)
    inner = both[:, :, :, 160:176].reshape(8, RANK, WIDE)
    outer = both[:, :, :, 176:, :80].reshape(2, 4, RANK, 8, 10)
    outer = outer.transpose(2, 3, 1, 0, 4).reshape(RANK, CH)
    return weight, inner, outer


def dot_last(left, right):
    return lax.dot_general(left, right, (((1,), (1,)), ((), ())), preferred_element_type=F32)


def dot_first(left, right):
    return lax.dot_general(left, right, (((0,), (0,)), ((), ())), preferred_element_type=F32)


def reduced(term_in, term_out):
    outer = jnp.pad(term_out, ((0, 0), (0, 1024 - CH))).reshape(RANK, 8, 128).transpose(1, 0, 2)
    slots = jnp.concatenate([term_in, outer], axis=2).reshape(2, 4, RANK, SLOT)
    slots = exchange(slots, ("c",)).sum(0)
    part = slots.reshape(16, 16, SLOT)
    part = exchange(part, ("y", "x")).sum(0)
    part = exchange(part.reshape(16, SLOT // 128, 128), Z).sum(0)
    return part


def spread(part):
    part = gather(part, Z).reshape(16, SLOT)
    full = gather(part, ("c", "y", "x")).reshape(8, RANK, SLOT)
    inner = full[:, :, :WIDE]
    outer = full[:, :, WIDE:].transpose(1, 0, 2).reshape(RANK, 1024)[:, :CH]
    return inner, outer


def per_device(acts, conv_weight, conv_bias, out_cotangent, basis_in, basis_out, query_ids):
    positions = 256
    ext = jnp.pad(halo(acts[0]), ((0, 0), (1, 1), (0, 0)))
    weight, inner, outer = gather_weights(conv_weight, basis_in, basis_out)
    patches = jnp.stack(
        [ext[a : a + 4, b : b + 64] for a in range(3) for b in range(3)], axis=2
    ).reshape(positions, 8, 4, 2, ROWS)
    patches = patches.transpose(3, 2, 0, 1, 4).reshape(8, positions, 8 * ROWS)
    patches = jnp.pad(patches, ((0, 0), (0, 0), (0, WIDE - 8 * ROWS)))
    blocks = [patches[k] for k in range(8)]

    preact = sum(dot_last(blocks[k], weight[k]) for k in range(8)) + conv_bias
    sigmoid_pre = jax.nn.sigmoid(preact)
    activated = (preact * sigmoid_pre).astype(BF16).reshape(acts.shape)
    cot = out_cotangent.reshape(positions, CH).astype(F32)
    grad_pre = (cot * sigmoid_pre * (1.0 + preact * (1.0 - sigmoid_pre))).astype(BF16)
    probe_in = sum(dot_last(blocks[k], inner[k]) for k in range(8)).astype(BF16)
    probe_out = dot_last(grad_pre, outer).astype(BF16)
    term_in = jnp.stack([dot_first(probe_in, blocks[k]) for k in range(8)])
    term_out = dot_first(probe_out, grad_pre)

    total = 131072.0
    fresh = (reduced(term_in, term_out) / total).astype(BF16)
    new_in, new_out = spread(fresh)

    square_in = jnp.sum(jnp.square(new_in.astype(F32)), axis=(0, 2))
    square_out = jnp.sum(jnp.square(new_out.astype(F32)), axis=1)
    scale_in, scale_out = jnp.sqrt(square_in), jnp.sqrt(square_out)
    raw_in = sum(dot_last(blocks[k], new_in[k]) for k in range(8))
    raw_out = dot_last(grad_pre, new_out)
    feat_in = (raw_in / scale_in).astype(BF16)
    feat_out = (raw_out / scale_out).astype(BF16)
    partial = dot_first(feat_out, feat_in) / 32

    zl, y, c, x = (lax.axis_index(a) for a in ("zl", "y", "c", "x"))
    quarter = partial.reshape(4, 8, 128)
    sent = jnp.broadcast_to(quarter[None], (8, 4, 8, 128)).reshape(32, 8, 128)
    got = exchange(lax.optimization_barrier(sent), ("y", "c", "x"))
    near = got.reshape(8, 4, 8, 128).sum(1)
    every = gather(near, Z).reshape(2, 8, 8, 8, 128).sum(0).reshape(64, 8, 128)
    mine = lax.dynamic_index_in_dim(every, lax.axis_index(BATCH), axis=0, keepdims=False)
    scale = scale_out[:, None] * scale_in[None, :] + DAMPING
    scale = lax.dynamic_slice_in_dim(scale, x * 16, 16, axis=0).reshape(8, 128)
    queries = jnp.take(every, query_ids, axis=0)
    scores = jnp.sum(queries * (mine / scale)[None], axis=(1, 2)) / (RANK * math.sqrt(RANK))
    scores = jnp.broadcast_to(scores[:, None], (8, 128))
    scores = gather(scores, ("x",)).reshape(4, 8, 128).sum(0)[:, :1]

    row = lax.dynamic_index_in_dim(new_in, c * 4 + y, axis=0, keepdims=False)
    basis_in_new = lax.dynamic_slice_in_dim(row[:, : 8 * ROWS], zl * ROWS, ROWS, axis=1).T
    return (activated, basis_in_new, scores)


def solution(mesh):
    inner = Mesh(mesh.devices.reshape([n for _, n in SPLIT]), AXES)
    return jax.shard_map(
        per_device,
        mesh=inner,
        in_specs=(
            P(BATCH, SPACE, None, None),
            P(BATCH, SPACE),
            P(),
            P(BATCH, SPACE, None, None),
            P(BATCH, None),
            P(BATCH, None),
            P(),
        ),
        out_specs=(P(BATCH, SPACE, None, None), P(BATCH, None), P(None, BATCH)),
        check_vma=False,
    )
```

time: 1850 us -> 324 us (0.18)
  the two profiles are of different devices: /device:TPU:1 before, /device:TPU:32 now
where the time goes in v1:
time: 324 us; the launch traced here: 323 us
  blocking collectives  140 us (43%)
  local copies, waits for them, and re-layouts  74.6 us (23%)
  waiting for transfers between devices  54.6 us (17%)
  starting transfers between devices  23.7 us (7%)
  matrix products  23.5 us (7%)
  other arithmetic  4.63 us (1%)
    all_to_all x8, blocking collectives, exchange(): return lax.all_to_all(value, axes, 0, 0, tiled=True)  140 us
    all_to_all x3, waiting for transfers between devices, exchange(): return lax.all_to_all(value, axes, 0, 0, tiled=True)  34.3 us
    slice x9, local copies, waits for them, and re-layouts, per_device(): blocks = [patches[k] for k in range(8)]  25.8 us
    dot_general x24, matrix products, dot_last(): lax.dot_general(left, right, (((1,), (1,)), ((), ())), preferred_element_...  18.4 us
    ppermute x1, waiting for transfers between devices, halo(): after = lax.ppermute(value[:1], SPACE, down)  16.8 us
    all_to_all x3, starting transfers between devices, exchange(): return lax.all_to_all(value, axes, 0, 0, tiled=True)  15.1 us
    broadcast_in_dim x6, local copies, waits for them, and re-layouts, gather(): copies = jnp.broadcast_to(value[None], (count,) + value.shape)  10.6 us
    another operation x2, local copies, waits for them, and re-layouts, per_device(): jnp.stack([ext[a:a + 4, b:b + 64] for a in range(3) for b in range(3)], a...  8.28 us
  transfers between devices with their start and end apart: 5, of which 4 were waited for; matrix products, arithmetic and copies ran while one was open for 16% of the time, Pallas kernels for 0%

profile of v1, /device:TPU:32, one launch (start us, length us, event | category | flops | bytes accessed | tf_op | source)
XLA Modules:
  0.0 322.9 jit_solution(11316813068203672150)
XLA Ops:
  3.5 36.0 %all_to_all.55 = bf16[16,88,128]{2,1,0:T(8,128)(2,1)S(1)} all-to-all(bf16[16,88,128]{2,1,0:T(8,128)(2,1)S(1)} %broadcast_in_dim.27), channel_id=1, replica_groups=mesh['zl'=8,'y'=4,'c'=2,'x'=4,'zh'=2] {'zh','zl'}, dimensions={0} | all-to-all | bytes 720896 | tf_op jit(solution)/shard_map/all_to_all | solution.py:27
  40.3 2.6 broadcast_in_dim.28
  42.8 7.2 %all-to-all-start.1 = ((bf16[16,192,768]{2,1,0:T(8,128)(2,1)}), bf16[16,192,768]{2,1,0:T(8,128)(2,1)}, u32[]{:S(2)}, u32[]{:S(2)}) async-start(bf16[16,192,768]{2,1,0:T(8,128)(2,1)} %broadcast_in_dim.28), calls=%async_computation.1 | async-start | bytes 9437184 | tf_op jit(solution)/shard_map/all_to_all | solution.py:27
  50.1 7.4 %collective-permute-start = (bf16[1,64,640]{2,1,0:T(8,128)(2,1)S(1)}, bf16[1,64,640]{2,1,0:T(8,128)(2,1)S(1)}, u32[]{:S(2)}, u32[]{:S(2)}) collective-permute-start(bf16[1,64,640]{2,1,0:T(8,128)(2,1)S(1)} %get-tuple-element.16), channel_id=1, source_target_pairs={{0,1},{1,2},{2,3},{3,4},{4,5},{5,6},{6,7},{8,9},{9,10},{10,11},{11... | collective-permute-start | bytes 245768 | tf_op jit(solution)/shard_map/ppermute | solution.py:39
  58.8 3.5 %collective-permute-done = bf16[1,64,640]{2,1,0:T(8,128)(2,1)S(1)} collective-permute-done((bf16[1,64,640]{2,1,0:T(8,128)(2,1)S(1)}, bf16[1,64,640]{2,1,0:T(8,128)(2,1)S(1)}, u32[]{:S(2)}, u32[]{:S(2)}) %collective-permute-start) | collective-permute-done | bytes 81952 | tf_op jit(solution)/shard_map/ppermute | solution.py:39
  62.3 16.8 %collective-permute-done.1 = bf16[1,64,640]{2,1,0:T(8,128)(2,1)S(1)} collective-permute-done((bf16[1,64,640]{2,1,0:T(8,128)(2,1)S(1)}, bf16[1,64,640]{2,1,0:T(8,128)(2,1)S(1)}, u32[]{:S(2)}, u32[]{:S(2)}) %collective-permute-start.1) | collective-permute-done | bytes 81952 | tf_op jit(solution)/shard_map/ppermute | solution.py:40
  79.8 8.2 %copy.35 = bf16[4,64,9,640]{1,0,3,2:T(4,128)(2,1)} copy(bf16[4,64,9,640]{3,1,0,2:T(8,128)(2,1)S(1)} %fusion.61) | data formatting | bytes 5898240 | tf_op jit(solution)/shard_map/stack | solution.py:104
  88.0 7.3 %reshape.112 = bf16[256,8,4,2,90]{0,4,3,2,1:T(8,128)(2,1)S(1)} reshape(bf16[4,64,9,640]{1,0,3,2:T(4,128)(2,1)} %copy.35) | data formatting | bytes 5898240 | tf_op jit(solution)/shard_map/reshape | solution.py:106
  95.3 3.9 %copy.36 = bf16[2,4,256,8,90]{2,1,0,4,3:T(4,128)(2,1)} copy(bf16[2,4,256,8,90]{2,4,0,1,3:T(8,128)(2,1)S(1)} %bitcast.311) | data formatting | bytes 5898240 | tf_op jit(solution)/shard_map/transpose | solution.py:107
  99.2 4.3 %reshape.113 = bf16[8,256,720]{1,0,2:T(8,128)(2,1)S(1)} reshape(bf16[2,4,256,8,90]{2,1,0,4,3:T(4,128)(2,1)} %copy.36) | data formatting | bytes 5898240 | tf_op jit(solution)/shard_map/reshape | solution.py:107
  103.6 8.6 %pad_slice_fusion = (bf16[1,256,768]{1,0,2:T(2,128)(2,1)}, bf16[1,256,768]{1,0,2:T(2,128)(2,1)}, bf16[1,256,768]{1,0,2:T(2,128)(2,1)}, bf16[1,256,768]{1,0,2:T(2...) fusion(bf16[8,256,720]{1,0,2:T(8,128)(2,1)S(1)} %reshape.113), kind=kLoop, calls=%fused_computation.13 | loop fusion | bytes 6094848 | tf_op jit(solution)/shard_map/slice | solution.py:109
  112.2 3.0 copy.48
  115.2 3.0 copy.42
  118.2 3.0 copy.43
  121.1 2.9 copy.44
  129.5 7.0 %broadcast_in_dim.29 = bf16[2,16,192,768]{3,2,1,0:T(8,128)(2,1)} broadcast(bf16[16,192,768]{2,1,0:T(8,128)(2,1)} %all-to-all-done.1), dimensions={1,2,3} | broadcast | bytes 14155776 | tf_op jit(solution)/shard_map/broadcast_in_dim | solution.py:32
  136.5 13.0 %all_to_all.56 = bf16[2,16,192,768]{3,2,1,0:T(8,128)(2,1)S(1)} all-to-all(bf16[2,16,192,768]{3,2,1,0:T(8,128)(2,1)} %broadcast_in_dim.29), channel_id=1, replica_groups=mesh['zl'=8,'y'=4,'c'=2,'x'=4,'zh'=2] {'c'}, dimensions={0} | all-to-all | bytes 18874368 | tf_op jit(solution)/shard_map/all_to_all | solution.py:27
  151.2 3.7 %slice.245 = bf16[2,4,4,160,768]{4,3,2,1,0:T(8,128)(2,1)} slice(bf16[2,4,4,192,768]{4,3,2,1,0:T(8,128)(2,1)S(1)} %bitcast.302), slice={[0:2], [0:4], [0:4], [0:160], [0:768]} | slice | bytes 15728640 | tf_op jit(solution)/shard_map/slice | solution.py:67
  158.2 1.9 fusion.15
  164.7 1.8 convolution_add_fusion.5
  172.4 2.2 fusion.13
  177.3 6.1 %all_to_all.57 = f32[2,4,64,896]{3,2,1,0:T(8,128)} all-to-all(f32[2,4,64,896]{3,2,1,0:T(8,128)S(1)} %bitcast.323), channel_id=1, replica_groups=mesh['zl'=8,'y'=4,'c'=2,'x'=4,'zh'=2] {'c'}, dimensions={0} | all-to-all | bytes 3670016 | tf_op jit(solution)/shard_map/all_to_all | solution.py:27
  183.4 2.7 reduce_sum.81
  186.0 19.9 %all_to_all.58 = f32[16,16,896]{2,1,0:T(8,128)S(1)} all-to-all(f32[16,16,896]{2,1,0:T(8,128)} %bitcast.327), channel_id=1, replica_groups=mesh['zl'=8,'y'=4,'c'=2,'x'=4,'zh'=2] {'y','x'}, dimensions={0} | all-to-all | bytes 1835008 | tf_op jit(solution)/shard_map/all_to_all | solution.py:27
  206.0 20.0 %all_to_all.59 = f32[16,7,128]{2,1,0:T(8,128)S(1)} all-to-all(f32[16,7,128]{2,1,0:T(8,128)S(1)} %reshape.127), channel_id=1, replica_groups=mesh['zl'=8,'y'=4,'c'=2,'x'=4,'zh'=2] {'zh','zl'}, dimensions={0} | all-to-all | bytes 114688 | tf_op jit(solution)/shard_map/all_to_all | solution.py:27
  226.1 15.3 %all_to_all.60 = bf16[16,7,128]{2,1,0:T(8,128)(2,1)S(1)} all-to-all(bf16[16,7,128]{2,1,0:T(8,128)(2,1)S(1)} %broadcast_in_dim.30), channel_id=1, replica_groups=mesh['zl'=8,'y'=4,'c'=2,'x'=4,'zh'=2] {'zh','zl'}, dimensions={0} | all-to-all | bytes 57344 | tf_op jit(solution)/shard_map/all_to_all | solution.py:27
  241.4 19.5 %all_to_all.61 = bf16[32,16,896]{2,1,0:T(8,128)(2,1)S(1)} all-to-all(bf16[32,16,896]{2,1,0:T(8,128)(2,1)S(1)} %broadcast_in_dim.32), channel_id=1, replica_groups=mesh['zl'=8,'y'=4,'c'=2,'x'=4,'zh'=2] {'c','y','x'}, dimensions={0} | all-to-all | bytes 1835008 | tf_op jit(solution)/shard_map/all_to_all | solution.py:27
  266.0 10.6 %all_to_all.62 = f32[32,8,128]{2,1,0:T(8,128)S(1)} all-to-all(f32[32,8,128]{2,1,0:T(8,128)S(1)} %bitcast.341), channel_id=1, replica_groups=mesh['zl'=8,'y'=4,'c'=2,'x'=4,'zh'=2] {'y','c','x'}, dimensions={0} | all-to-all | bytes 262144 | tf_op jit(solution)/shard_map/all_to_all | solution.py:27
  277.5 4.6 %all-to-all-start.9 = ((f32[16,8,8,128]{3,2,1,0:T(8,128)}), f32[16,8,8,128]{3,2,1,0:T(8,128)S(1)}, u32[]{:S(2)}, u32[]{:S(2)}) async-start(f32[16,8,8,128]{3,2,1,0:T(8,128)} %broadcast_in_dim.72), calls=%async_computation.9 | async-start | bytes 1048576 | tf_op jit(solution)/shard_map/all_to_all | solution.py:27
  282.5 29.7 %all-to-all-done.9 = f32[16,8,8,128]{3,2,1,0:T(8,128)S(1)} async-done(((f32[16,8,8,128]{3,2,1,0:T(8,128)}), f32[16,8,8,128]{3,2,1,0:T(8,128)S(1)}, u32[]{:S(2)}, u32[]{:S(2)}) %all-to-all-start.9) | async-done | bytes 524320 | tf_op jit(solution)/shard_map/all_to_all | solution.py:27
  313.7 3.2 %all-to-all-start.10 = ((f32[4,8,128]{2,1,0:T(8,128)}), f32[4,8,128]{2,1,0:T(8,128)S(1)}, u32[]{:S(2)}, u32[]{:S(2)}) async-start(f32[4,8,128]{2,1,0:T(8,128)} %broadcast_in_dim_broadcast_in_dim_broadcast_in_dim.2), calls=%async_computation.10 | async-start | bytes 32768 | tf_op jit(solution)/shard_map/all_to_all | solution.py:27
  317.6 4.6 %all-to-all-done.10 = f32[4,8,128]{2,1,0:T(8,128)S(1)} async-done(((f32[4,8,128]{2,1,0:T(8,128)}), f32[4,8,128]{2,1,0:T(8,128)S(1)}, u32[]{:S(2)}, u32[]{:S(2)}) %all-to-all-start.10) | async-done | bytes 16416 | tf_op jit(solution)/shard_map/all_to_all | solution.py:27
  (145 shorter events, 38.1 us)
Async XLA Ops:
  0.6 0.7 copy-start
  42.8 7.2 %copy-start.9 = (bf16[1,4,64,640]{3,2,1,0:T(8,128)(2,1)S(1)}, bf16[1,4,64,640]{3,2,1,0:T(8,128)(2,1)}, u32[]{:S(2)}) copy-start(bf16[1,4,64,640]{3,2,1,0:T(8,128)(2,1)} %param.7) | copy-start | bytes 983044
  42.8 86.6 %all-to-all-start.1 = ((bf16[16,192,768]{2,1,0:T(8,128)(2,1)}), bf16[16,192,768]{2,1,0:T(8,128)(2,1)}, u32[]{:S(2)}, u32[]{:S(2)}) async-start(bf16[16,192,768]{2,1,0:T(8,128)(2,1)} %broadcast_in_dim.28), calls=%async_computation.1 | async-start | bytes 9437184 | tf_op jit(solution)/shard_map/all_to_all | solution.py:27
  50.1 12.2 %collective-permute-start = (bf16[1,64,640]{2,1,0:T(8,128)(2,1)S(1)}, bf16[1,64,640]{2,1,0:T(8,128)(2,1)S(1)}, u32[]{:S(2)}, u32[]{:S(2)}) collective-permute-start(bf16[1,64,640]{2,1,0:T(8,128)(2,1)S(1)} %get-tuple-element.16), channel_id=1, source_target_pairs={{0,1},{1,2},{2,3},{3,4},{4,5},{5,6},{6,7},{8,9},{9,10},{10,11},{11... | collective-permute-start | bytes 245768 | tf_op jit(solution)/shard_map/ppermute | solution.py:39
  57.5 21.6 %collective-permute-start.1 = (bf16[1,64,640]{2,1,0:T(8,128)(2,1)S(1)}, bf16[1,64,640]{2,1,0:T(8,128)(2,1)S(1)}, u32[]{:S(2)}, u32[]{:S(2)}) collective-permute-start(bf16[1,64,640]{2,1,0:T(8,128)(2,1)S(1)} %get-tuple-element.17), channel_id=1, source_target_pairs={{1,0},{2,1},{3,2},{4,3},{5,4},{6,5},{7,6},{9,8},{10,9},{11,10},{12... | collective-permute-start | bytes 245768 | tf_op jit(solution)/shard_map/ppermute | solution.py:40
  112.2 11.8 %copy-start.15 = (bf16[1,256,768]{1,0,2:T(2,128)(2,1)S(1)}, bf16[1,256,768]{1,0,2:T(2,128)(2,1)}, u32[]{:S(2)}) copy-start(bf16[1,256,768]{1,0,2:T(2,128)(2,1)} %get-tuple-element.10) | copy-start | bytes 1179652
  112.2 13.4 %copy-start.14 = (bf16[1,256,768]{1,0,2:T(2,128)(2,1)S(1)}, bf16[1,256,768]{1,0,2:T(2,128)(2,1)}, u32[]{:S(2)}) copy-start(bf16[1,256,768]{1,0,2:T(2,128)(2,1)} %get-tuple-element.11) | copy-start | bytes 1179652
  115.2 12.2 %copy-start.13 = (bf16[1,256,768]{1,0,2:T(2,128)(2,1)S(1)}, bf16[1,256,768]{1,0,2:T(2,128)(2,1)}, u32[]{:S(2)}) copy-start(bf16[1,256,768]{1,0,2:T(2,128)(2,1)} %get-tuple-element.12) | copy-start | bytes 1179652
  118.2 9.7 %copy-start.12 = (bf16[1,256,768]{1,0,2:T(2,128)(2,1)S(1)}, bf16[1,256,768]{1,0,2:T(2,128)(2,1)}, u32[]{:S(2)}) copy-start(bf16[1,256,768]{1,0,2:T(2,128)(2,1)} %get-tuple-element.13) | copy-start | bytes 1179652
  154.9 3.3 %copy-start.8 = (bf16[1,256,768]{2,1,0:T(8,128)(2,1)S(1)}, bf16[1,256,768]{2,1,0:T(8,128)(2,1)}, u32[]{:S(2)}) copy-start(bf16[1,256,768]{2,1,0:T(8,128)(2,1)} %copy.37) | copy-start | bytes 1179652
  154.9 5.2 %copy-start.7 = (bf16[1,256,768]{2,1,0:T(8,128)(2,1)S(1)}, bf16[1,256,768]{2,1,0:T(8,128)(2,1)}, u32[]{:S(2)}) copy-start(bf16[1,256,768]{2,1,0:T(8,128)(2,1)} %copy.42) | copy-start | bytes 1179652
  156.9 6.6 %copy-start.6 = (bf16[1,256,768]{2,1,0:T(8,128)(2,1)S(1)}, bf16[1,256,768]{2,1,0:T(8,128)(2,1)}, u32[]{:S(2)}) copy-start(bf16[1,256,768]{2,1,0:T(8,128)(2,1)} %copy.43) | copy-start | bytes 1179652
  158.2 9.4 %copy-start.2 = (bf16[2,4,4,160,768]{4,3,2,1,0:T(8,128)(2,1)S(1)}, bf16[2,4,4,160,768]{4,3,2,1,0:T(8,128)(2,1)}, u32[]{:S(2)}) copy-start(bf16[2,4,4,160,768]{4,3,2,1,0:T(8,128)(2,1)} %slice.245) | copy-start | bytes 23592964
  161.7 4.8 %copy-start.5 = (bf16[1,256,768]{2,1,0:T(8,128)(2,1)S(1)}, bf16[1,256,768]{2,1,0:T(8,128)(2,1)}, u32[]{:S(2)}) copy-start(bf16[1,256,768]{2,1,0:T(8,128)(2,1)} %copy.44) | copy-start | bytes 1179652
  164.7 3.5 %copy-start.4 = (bf16[1,256,768]{2,1,0:T(8,128)(2,1)S(1)}, bf16[1,256,768]{2,1,0:T(8,128)(2,1)}, u32[]{:S(2)}) copy-start(bf16[1,256,768]{2,1,0:T(8,128)(2,1)} %copy.45) | copy-start | bytes 1179652
  164.7 3.5 %copy-start.16 = (bf16[2,4,4,16,768]{4,3,2,1,0:T(8,128)(2,1)S(1)}, bf16[2,4,4,16,768]{4,3,2,1,0:T(8,128)(2,1)}, u32[]{:S(2)}) copy-start(bf16[2,4,4,16,768]{4,3,2,1,0:T(8,128)(2,1)} %slice.254) | copy-start | bytes 2359300
  167.7 1.3 copy-start.3
  169.2 1.3 copy-start.10
  169.3 1.6 copy-start.17
  169.3 1.6 copy-start.18
  261.0 3.4 %copy-start.11 = (bf16[1,256,768]{2,1,0:T(8,128)(2,1)S(1)}, bf16[1,256,768]{2,1,0:T(8,128)(2,1)}, u32[]{:S(2)}) copy-start(bf16[1,256,768]{2,1,0:T(8,128)(2,1)} %copy.48) | copy-start | bytes 1179652
  263.3 18.8 %copy-start.19 = (s32[8]{0:T(128)S(1)}, s32[8]{0:T(128)}, u32[]{:S(2)}) copy-start(s32[8]{0:T(128)} %param.13) | copy-start | bytes 100
  264.3 58.5 %copy-start.1 = (bf16[90,64]{0,1:T(8,128)(2,1)S(1)}, bf16[90,64]{0,1:T(8,128)(2,1)}, u32[]{:S(2)}) copy-start(bf16[90,64]{0,1:T(8,128)(2,1)} %param.11) | copy-start | bytes 34564
  277.5 34.6 %all-to-all-start.9 = ((f32[16,8,8,128]{3,2,1,0:T(8,128)}), f32[16,8,8,128]{3,2,1,0:T(8,128)S(1)}, u32[]{:S(2)}, u32[]{:S(2)}) async-start(f32[16,8,8,128]{3,2,1,0:T(8,128)} %broadcast_in_dim.72), calls=%async_computation.9 | async-start | bytes 1048576 | tf_op jit(solution)/shard_map/all_to_all | solution.py:27
  313.7 8.6 %all-to-all-start.10 = ((f32[4,8,128]{2,1,0:T(8,128)}), f32[4,8,128]{2,1,0:T(8,128)S(1)}, u32[]{:S(2)}, u32[]{:S(2)}) async-start(f32[4,8,128]{2,1,0:T(8,128)} %broadcast_in_dim_broadcast_in_dim_broadcast_in_dim.2), calls=%async_computation.10 | async-start | bytes 32768 | tf_op jit(solution)/shard_map/all_to_all | solution.py:27

commit v2 on v1

v2 whole, which is shorter than its diff:
```python
import math

import jax
import jax.numpy as jnp
from jax import lax
from jax.experimental import pallas as pl
from jax.experimental.pallas import tpu as pltpu
from jax.sharding import Mesh
from jax.sharding import PartitionSpec as P

DAMPING = 0.1
SPLIT = (("zl", 8), ("y", 4), ("c", 2), ("x", 4), ("zh", 2))
AXES = tuple(name for name, _ in SPLIT)
SIZES = dict(SPLIT)
BATCH = ("zl", "y", "c")
SPACE = ("x", "zh")
Z = ("zh", "zl")
F32, BF16 = jnp.float32, jnp.bfloat16

CH, RANK, TAPS = 640, 64, 9
PATCH = TAPS * CH
ROWS = PATCH // 64
COLS = CH // 8
WIDE = 768
SLOT = WIDE + 128


def exchange(value, axes):
    return lax.all_to_all(value, axes, 0, 0, tiled=True)


def gather(value, axes):
    count = math.prod(SIZES[a] for a in axes)
    copies = jnp.broadcast_to(value[None], (count,) + value.shape)
    return exchange(lax.optimization_barrier(copies), axes)


def halo(value):
    up = [(i, i + 1) for i in range(7)]
    down = [(j, i) for i, j in up]
    return lax.ppermute(value[-1:], SPACE, up), lax.ppermute(value[:1], SPACE, down)


def gather_weights(conv_weight, basis_in, basis_out):
    at = lax.axis_index(SPACE) * 8
    kernel = conv_weight.T
    basis = lax.dynamic_slice_in_dim(basis_in.T, at, 8, axis=0)
    outer = lax.dynamic_slice_in_dim(basis_out.T, at, 8, axis=0)
    rows = jnp.pad(jnp.concatenate([kernel, basis], axis=0), ((0, 0), (0, 128 - ROWS)))
    rows = lax.dynamic_update_slice(rows, outer, (COLS, ROWS))
    got = gather(rows, Z).reshape(2, 8, COLS + 8, 128)

    def merged(part, width):
        flat = part.transpose(0, 2, 1, 3).reshape(part.shape[0] * part.shape[2], -1)
        return jnp.pad(flat, ((0, 0), (0, WIDE - flat.shape[1])))

    joined = jnp.concatenate(
        [
            merged(got[:, :, :COLS, :ROWS], ROWS),
            merged(got[:, :, COLS:, :ROWS], ROWS),
            merged(got[:, :, COLS:, ROWS : ROWS + 10], 10),
        ],
        axis=0,
    )
    return gather(joined, ("y", "x"))


def swap(value):
    return lax.ppermute(value, "c", [(0, 1), (1, 0)])


def dot_last(left, right):
    return lax.dot_general(left, right, (((1,), (1,)), ((), ())), preferred_element_type=F32)


def dot_plain(left, right):
    return jnp.dot(left, right, preferred_element_type=F32)


def vmem():
    return pl.BlockSpec(memory_space=pltpu.VMEM)


def patch_kernel(before, band, after, out, flat):
    row = lax.broadcasted_iota(jnp.int32, (64, CH), 0)
    for line in range(6):
        value = before[0] if line == 0 else after[0] if line == 5 else band[line - 1]
        wide = value.astype(F32)
        left = jnp.where(row == 0, 0.0, pltpu.roll(wide, 1, 0)).astype(BF16)
        right = jnp.where(row == 63, 0.0, pltpu.roll(wide, 63, 0)).astype(BF16)
        for tap_row in range(3):
            at = line - tap_row
            if 0 <= at < 4:
                for tap_col, moved in enumerate((left, value, right)):
                    tap = tap_row * 3 + tap_col
                    flat[at * 64 : at * 64 + 64, tap * CH : tap * CH + CH] = moved
    for c in range(2):
        for y in range(4):
            starts = [(zl * 8 + y * 2 + c) * ROWS for zl in range(8)]
            pieces = [flat[:, k : k + ROWS] for k in starts]
            pieces.append(jnp.zeros((256, WIDE - 8 * ROWS), BF16))
            out[c, y] = jnp.concatenate(pieces, axis=1)


def build_patches(before, band, after):
    return pl.pallas_call(
        patch_kernel,
        out_shape=jax.ShapeDtypeStruct((2, 4, 256, WIDE), BF16),
        in_specs=[vmem()] * 3,
        out_specs=vmem(),
        scratch_shapes=[pltpu.VMEM((256, PATCH), BF16)],
    )(before, band, after)


def first_kernel(
    core, own, other, patches, bias, cot, act, grad, kept, sent, total, outer, chunks
):
    y = pl.program_id(0)
    me = core[0]

    @pl.when(y == 0)
    def _():
        total[...] = jnp.zeros_like(total)
        outer[...] = jnp.zeros_like(outer)

    k = lax.broadcasted_iota(jnp.int32, (128, CH), 0)
    n = lax.broadcasted_iota(jnp.int32, (128, CH), 1)
    tens = lax.shift_right_logical(k * 6554, 16)
    spot = n - (tens * 80 + k - tens * 10)
    for c, half in ((me, own), (1 - me, other)):
        weight = half[...].reshape(WIDE, WIDE)
        total[...] += dot_last(patches[c, y], weight)
        piece = jnp.concatenate([half[x, 176:192, :128] for x in range(4)], axis=0)
        pick = jnp.where(spot == y * 20 + c * 10, 1.0, 0.0).astype(BF16)
        outer[...] += dot_plain(piece, pick)

    @pl.when(y == 3)
    def _():
        pre = jnp.concatenate([total[:, x * 192 : x * 192 + 160] for x in range(4)], axis=1)
        probe = jnp.concatenate(
            [total[:, x * 192 + 160 : x * 192 + 176] for x in range(4)], axis=1
        )
        pre = pre + bias[...]
        sig = jax.nn.sigmoid(pre)
        act[...] = (pre * sig).astype(BF16)
        slope = cot[...].astype(F32) * sig * (1.0 + pre * (1.0 - sig))
        grads = slope.astype(BF16)
        grad[...] = grads
        probe_in = probe.T.astype(BF16)
        probe_out = dot_last(outer[...].astype(BF16), grads).astype(BF16)
        term_out = dot_plain(probe_out, grads)
        for j in range(8):
            chunks[j] = term_out[:, j * 128 : j * 128 + 128] if j < 5 else jnp.zeros((RANK, 128), F32)
        for c, dest in ((me, kept), (1 - me, sent)):
            for at in range(4):
                dest[at, :, :WIDE] = dot_plain(probe_in, patches[c, at])
                dest[at, :, WIDE:] = chunks[c * 4 + at]


def first_pass(core, own, other, patches, bias, cot):
    half = pl.BlockSpec((4, 192, WIDE), lambda y, core: (y, 0, 0))

    def whole(*shape):
        return pl.BlockSpec(shape, lambda y, core: (0,) * len(shape))

    return pl.pallas_call(
        first_kernel,
        grid_spec=pltpu.PrefetchScalarGridSpec(
            num_scalar_prefetch=1,
            grid=(4,),
            in_specs=[half, half, whole(2, 4, 256, WIDE), whole(1, CH), whole(256, CH)],
            out_specs=[
                whole(256, CH),
                whole(256, CH),
                whole(4, RANK, SLOT),
                whole(4, RANK, SLOT),
            ],
            scratch_shapes=[
                pltpu.VMEM((256, WIDE), F32),
                pltpu.VMEM((RANK, CH), F32),
                pltpu.VMEM((8, RANK, 128), F32),
            ],
        ),
        out_shape=[
            jax.ShapeDtypeStruct((256, CH), BF16),
            jax.ShapeDtypeStruct((256, CH), BF16),
            jax.ShapeDtypeStruct((4, RANK, SLOT), F32),
            jax.ShapeDtypeStruct((4, RANK, SLOT), F32),
        ],
    )(core, own, other, patches, bias, cot)


def second_kernel(full, patches, grad, partial, scale_in, scale_out):
    raw_in = jnp.zeros((RANK, 256), F32)
    raw_out = jnp.zeros((RANK, 256), F32)
    square_in = jnp.zeros((RANK, 1), F32)
    square_out = jnp.zeros((RANK, 1), F32)
    for j in range(8):
        block = full[j, :, :WIDE]
        raw_in += dot_last(block, patches[j // 4, j % 4])
        square_in += jnp.sum(jnp.square(block.astype(F32)), axis=1, keepdims=True)
        if j < 5:
            chunk = full[j, :, WIDE:]
            raw_out += dot_last(chunk, grad[:, j * 128 : j * 128 + 128])
            square_out += jnp.sum(jnp.square(chunk.astype(F32)), axis=1, keepdims=True)
    root_in, root_out = jnp.sqrt(square_in), jnp.sqrt(square_out)
    feat_in = (raw_in / root_in).astype(BF16)
    feat_out = (raw_out / root_out).astype(BF16)
    partial[...] = dot_last(feat_out, feat_in) * (1.0 / 32)
    scale_in[...] = root_in
    scale_out[...] = root_out


def second_pass(full, patches, grad):
    return pl.pallas_call(
        second_kernel,
        out_shape=[
            jax.ShapeDtypeStruct((RANK, RANK), F32),
            jax.ShapeDtypeStruct((RANK, 1), F32),
            jax.ShapeDtypeStruct((RANK, 1), F32),
        ],
        in_specs=[vmem()] * 3,
        out_specs=[vmem()] * 3,
    )(full, patches, grad)


def reduced(kept, sent):
    part = (kept + swap(sent)).reshape(16, 16, SLOT)
    part = exchange(part, ("y", "x")).sum(0)
    return exchange(part.reshape(16, SLOT // 128, 128), Z).sum(0)


def spread(part):
    part = gather(part, Z).reshape(16, SLOT)
    return gather(part, ("c", "y", "x")).reshape(8, RANK, SLOT)


def per_device(acts, conv_weight, conv_bias, out_cotangent, basis_in, basis_out, query_ids):
    before, after = halo(acts[0])
    own = gather_weights(conv_weight, basis_in, basis_out)
    patches = build_patches(before, acts[0], after)
    core = lax.axis_index("c").astype(jnp.int32).reshape(1)
    activated, grad_pre, kept, sent = first_pass(
        core, own, swap(own), patches, conv_bias.reshape(1, CH), out_cotangent.reshape(256, CH)
    )
    activated = activated.reshape(acts.shape)
    full = spread((reduced(kept, sent) / 131072.0).astype(BF16))
    partial, scale_in, scale_out = second_pass(full, patches, grad_pre)

    zl, y, c, x = (lax.axis_index(a) for a in ("zl", "y", "c", "x"))
    quarter = partial.reshape(4, 8, 128)
    sent = jnp.broadcast_to(quarter[None], (8, 4, 8, 128)).reshape(32, 8, 128)
    got = exchange(lax.optimization_barrier(sent), ("y", "c", "x"))
    near = got.reshape(8, 4, 8, 128).sum(1)
    every = gather(near, Z).reshape(2, 8, 8, 8, 128).sum(0).reshape(64, 8, 128)
    mine = lax.dynamic_index_in_dim(every, lax.axis_index(BATCH), axis=0, keepdims=False)
    scale = scale_out * scale_in.T + DAMPING
    scale = lax.dynamic_slice_in_dim(scale, x * 16, 16, axis=0).reshape(8, 128)
    queries = jnp.take(every, query_ids, axis=0)
    scores = jnp.sum(queries * (mine / scale)[None], axis=(1, 2)) / (RANK * math.sqrt(RANK))
    scores = jnp.broadcast_to(scores[:, None], (8, 128))
    scores = gather(scores, ("x",)).reshape(4, 8, 128).sum(0)[:, :1]

    row = lax.dynamic_index_in_dim(full, c * 4 + y, axis=0, keepdims=False)
    basis_in_new = lax.dynamic_slice_in_dim(row[:, : 8 * ROWS], zl * ROWS, ROWS, axis=1).T
    return (activated, basis_in_new, scores)


def solution(mesh):
    inner = Mesh(mesh.devices.reshape([n for _, n in SPLIT]), AXES)
    return jax.shard_map(
        per_device,
        mesh=inner,
        in_specs=(
            P(BATCH, SPACE, None, None),
            P(BATCH, SPACE),
            P(),
            P(BATCH, SPACE, None, None),
            P(BATCH, None),
            P(BATCH, None),
            P(),
        ),
        out_specs=(P(BATCH, SPACE, None, None), P(BATCH, None), P(None, BATCH)),
        check_vma=False,
    )
```

time: 324 us -> 291 us (0.90)
  local copies, waits for them, and re-layouts: 74.6 us -> 9.82 us
  blocking collectives: 140 us -> 181 us
  matrix products: 23.5 us -> 0 us
  Pallas kernels: 0 us -> 18.7 us
  starting transfers between devices: 23.7 us -> 20.1 us
    all_to_all x8 -> x7, blocking collectives: 140 us -> 181 us  [exchange(): return lax.all_to_all(value, axes, 0, 0, tiled=True)]
    slice x15 -> x2, local copies, waits for them, and re-layouts: 32.8 us -> 0.02 us  [the longest x1 0.02 us: halo(): value[:1]]
    dot_general x34 -> x0, matrix products: 23.5 us -> none  [the longest x24 18.4 us: dot_last(): lax.dot_general(left, right, (((1,), (1,)), ((), ())), preferred_element_...]
    pallas_call x0 -> x3, Pallas kernels: none -> 18.7 us  [the longest x1 9.97 us: first_pass(): pl.pallas_call(first_kernel, grid_spec=pltpu.PrefetchScalarGridSpec(num_s...]
    reshape x6 -> x2, local copies, waits for them, and re-layouts: 12.1 us -> 0.59 us  [the longest x1 0.58 us: per_device(): conv_bias.reshape(1, CH)]
    broadcast_in_dim x6 -> x5, local copies, waits for them, and re-layouts: 10.6 us -> 1.43 us  [gather(): copies = jnp.broadcast_to(value[None], (count,) + value.shape)]
    another operation x2 -> x0, local copies, waits for them, and re-layouts: 8.28 us -> none  [per_device(): jnp.stack([ext[a:a + 4, b:b + 64] for a in range(3) for b in range(3)], a...]
    all_to_all x3 -> x2, starting transfers between devices: 15.1 us -> 7.86 us  [exchange(): return lax.all_to_all(value, axes, 0, 0, tiled=True)]
  transfers between devices with their start and end apart: 5 -> 6, of which waited for: 4 -> 5; matrix products, arithmetic and copies ran while one was open for 16% -> 1% of each run, Pallas kernels for 0% -> 2%
where the time goes in v2:
time: 291 us; the launch traced here: 290 us
  blocking collectives  181 us (62%)
  waiting for transfers between devices  55.9 us (19%)
  starting transfers between devices  20.1 us (7%)
  Pallas kernels  18.7 us (6%)
  local copies, waits for them, and re-layouts  9.82 us (3%)
  other arithmetic  4.23 us (1%)
    all_to_all x7, blocking collectives, exchange(): return lax.all_to_all(value, axes, 0, 0, tiled=True)  181 us
    all_to_all x2, waiting for transfers between devices, exchange(): return lax.all_to_all(value, axes, 0, 0, tiled=True)  31.7 us
    ppermute x1, waiting for transfers between devices, halo(): lax.ppermute(value[:1], SPACE, down)  16.7 us
    pallas_call x1, Pallas kernels, first_pass(): pl.pallas_call(first_kernel, grid_spec=pltpu.PrefetchScalarGridSpec(num_s...  9.97 us
    all_to_all x2, starting transfers between devices, exchange(): return lax.all_to_all(value, axes, 0, 0, tiled=True)  7.86 us
    ppermute x1, starting transfers between devices, halo(): lax.ppermute(value[-1:], SPACE, up)  7.09 us
  transfers between devices with their start and end apart: 6, of which 5 were waited for; matrix products, arithmetic and copies ran while one was open for 1% of the time, Pallas kernels for 2%

profile of v2, /device:TPU:32, one launch (start us, length us, event | category | flops | bytes accessed | tf_op | source)
XLA Modules:
  0.0 290.4 jit_solution(17536189938107780649)
XLA Ops:
  0.7 0.7 copy-done
  1.4 0.8 dynamic-slice_bitcast_fusion.2
  2.2 0.7 fusion.8
  3.5 36.0 %all_to_all.45 = bf16[16,88,128]{2,1,0:T(8,128)(2,1)S(1)} all-to-all(bf16[16,88,128]{2,1,0:T(8,128)(2,1)S(1)} %broadcast_in_dim.28), channel_id=1, replica_groups=mesh['zl'=8,'y'=4,'c'=2,'x'=4,'zh'=2] {'zh','zl'}, dimensions={0} | all-to-all | bytes 720896 | tf_op jit(solution)/shard_map/all_to_all | solution.py:29
  40.7 63.5 %all_to_all.46.own = bf16[16,192,768]{2,1,0:T(8,128)(2,1)} all-to-all(bf16[16,192,768]{2,1,0:T(8,128)(2,1)S(1)} %broadcast_in_dim.29), channel_id=1, replica_groups=mesh['zl'=8,'y'=4,'c'=2,'x'=4,'zh'=2] {'y','x'}, dimensions={0} | all-to-all | bytes 9437184 | tf_op jit(solution)/shard_map/all_to_all | solution.py:29
  104.2 1.9 collective-permute-start
  106.2 7.1 %collective-permute-start.1 = (bf16[1,64,640]{2,1,0:T(8,128)(2,1)S(1)}, bf16[1,64,640]{2,1,0:T(8,128)(2,1)S(1)}, u32[]{:S(2)}, u32[]{:S(2)}) collective-permute-start(bf16[1,64,640]{2,1,0:T(8,128)(2,1)S(1)} %get-tuple-element.21), channel_id=1, source_target_pairs={{0,1},{1,2},{2,3},{3,4},{4,5},{5,6},{6,7},{8,9},{9,10},{10,11},{11... | collective-permute-start | bytes 245768 | tf_op jit(solution)/shard_map/ppermute | solution.py:41
  113.3 1.3 collective-permute-start.2
  115.2 4.8 %collective-permute-done.1.before = bf16[1,64,640]{2,1,0:T(8,128)(2,1)S(1)} collective-permute-done((bf16[1,64,640]{2,1,0:T(8,128)(2,1)S(1)}, bf16[1,64,640]{2,1,0:T(8,128)(2,1)S(1)}, u32[]{:S(2)}, u32[]{:S(2)}) %collective-permute-start.1) | collective-permute-done | bytes 81952 | tf_op jit(solution)/shard_map/ppermute | solution.py:41
  120.0 16.7 %collective-permute-done.2.after = bf16[1,64,640]{2,1,0:T(8,128)(2,1)S(1)} collective-permute-done((bf16[1,64,640]{2,1,0:T(8,128)(2,1)S(1)}, bf16[1,64,640]{2,1,0:T(8,128)(2,1)S(1)}, u32[]{:S(2)}, u32[]{:S(2)}) %collective-permute-start.2) | collective-permute-done | bytes 81952 | tf_op jit(solution)/shard_map/ppermute | solution.py:41
  137.4 4.6 %shard_map.94.patches = bf16[2,4,256,768]{3,2,1,0:T(8,128)(2,1)} custom-call(bf16[1,64,640]{2,1,0:T(8,128)(2,1)} %copy-done.2, bf16[4,64,640]{2,1,0:T(8,128)(2,1)} %bitcast.51, bf16[1,64,640]{2,1,0:T(8,128)(2,1)} %copy-done.3), custom_call_target="tpu_custom_call" | custom-call | tf_op jit(solution)/shard_map/pallas_call | solution.py:106
  142.0 10.0 %shard_map.95 = (bf16[256,640]{1,0:T(8,128)(2,1)}, bf16[256,640]{1,0:T(8,128)(2,1)}, f32[4,64,896]{2,1,0:T(8,128)}, f32[4,64,896]{2,1,0:T(8,128)}) custom-call(s32[1]{0:T(128)} %bitcast.core, bf16[16,192,768]{2,1,0:T(8,128)(2,1)} %all_to_all.46.own, bf16[16,192,768]{2,1,0:T(8,128)(2,1)} %collective-permute-done.other, ...), custom_call_target="tpu_custom_call" | custom-call | tf_op jit(solution)/shard_map/pallas_call | solution.py:166
  152.0 1.9 collective-permute-start.3
  153.9 2.6 collective-permute-done.3
  156.6 1.3 add.53
  157.8 18.9 %all_to_all.47 = f32[16,16,896]{2,1,0:T(8,128)S(1)} all-to-all(f32[16,16,896]{2,1,0:T(8,128)S(1)} %bitcast.46), channel_id=1, replica_groups=mesh['zl'=8,'y'=4,'c'=2,'x'=4,'zh'=2] {'y','x'}, dimensions={0} | all-to-all | bytes 1835008 | tf_op jit(solution)/shard_map/all_to_all | solution.py:29
  176.8 16.3 %all_to_all.48 = f32[16,7,128]{2,1,0:T(8,128)S(1)} all-to-all(f32[16,7,128]{2,1,0:T(8,128)S(1)} %reshape.86), channel_id=1, replica_groups=mesh['zl'=8,'y'=4,'c'=2,'x'=4,'zh'=2] {'zh','zl'}, dimensions={0} | all-to-all | bytes 114688 | tf_op jit(solution)/shard_map/all_to_all | solution.py:29
  193.2 15.3 %all_to_all.49 = bf16[16,7,128]{2,1,0:T(8,128)(2,1)S(1)} all-to-all(bf16[16,7,128]{2,1,0:T(8,128)(2,1)S(1)} %broadcast_in_dim.54), channel_id=1, replica_groups=mesh['zl'=8,'y'=4,'c'=2,'x'=4,'zh'=2] {'zh','zl'}, dimensions={0} | all-to-all | bytes 57344 | tf_op jit(solution)/shard_map/all_to_all | solution.py:29
  208.6 20.0 %all_to_all.50 = bf16[32,16,896]{2,1,0:T(8,128)(2,1)} all-to-all(bf16[32,16,896]{2,1,0:T(8,128)(2,1)S(1)} %broadcast_in_dim.56), channel_id=1, replica_groups=mesh['zl'=8,'y'=4,'c'=2,'x'=4,'zh'=2] {'c','y','x'}, dimensions={0} | all-to-all | bytes 1835008 | tf_op jit(solution)/shard_map/all_to_all | solution.py:29
  228.6 4.1 %shard_map.96 = (f32[64,64]{1,0:T(8,128)}, f32[64,1]{1,0:T(8,128)}, f32[64,1]{1,0:T(8,128)}) custom-call(bf16[8,64,896]{2,1,0:T(8,128)(2,1)} %bitcast.44, bf16[2,4,256,768]{3,2,1,0:T(8,128)(2,1)} %shard_map.94.patches, bf16[256,640]{1,0:T(8,128)(2,1)} %get-tuple-element.13.grad), custom_call_target="tpu_custom_call" | custom-call | tf_op jit(solution)/shard_map/pallas_call | solution.py:215
  232.7 0.8 broadcast_in_dim.58
  233.5 10.6 %all_to_all.51 = f32[32,8,128]{2,1,0:T(8,128)S(1)} all-to-all(f32[32,8,128]{2,1,0:T(8,128)S(1)} %bitcast.52), channel_id=1, replica_groups=mesh['zl'=8,'y'=4,'c'=2,'x'=4,'zh'=2] {'y','c','x'}, dimensions={0} | all-to-all | bytes 262144 | tf_op jit(solution)/shard_map/all_to_all | solution.py:29
  244.2 0.8 broadcast_in_dim.60
  245.0 4.6 %all-to-all-start.7 = ((f32[16,8,8,128]{3,2,1,0:T(8,128)}), f32[16,8,8,128]{3,2,1,0:T(8,128)S(1)}, u32[]{:S(2)}, u32[]{:S(2)}) async-start(f32[16,8,8,128]{3,2,1,0:T(8,128)} %broadcast_in_dim.60), calls=%async_computation.7 | async-start | bytes 1048576 | tf_op jit(solution)/shard_map/all_to_all | solution.py:29
  249.7 0.9 reduce
  250.5 0.9 reduce.1
  251.7 0.9 dynamic-slice_bitcast_fusion
  252.6 27.1 %all-to-all-done.7 = f32[16,8,8,128]{3,2,1,0:T(8,128)S(1)} async-done(((f32[16,8,8,128]{3,2,1,0:T(8,128)}), f32[16,8,8,128]{3,2,1,0:T(8,128)S(1)}, u32[]{:S(2)}, u32[]{:S(2)}) %all-to-all-start.7) | async-done | bytes 524320 | tf_op jit(solution)/shard_map/all_to_all | solution.py:29
  280.5 0.7 broadcast_in_dim_broadcast_in_dim_broadcast_in_dim.2
  281.2 3.2 %all-to-all-start.8 = ((f32[4,8,128]{2,1,0:T(8,128)}), f32[4,8,128]{2,1,0:T(8,128)S(1)}, u32[]{:S(2)}, u32[]{:S(2)}) async-start(f32[4,8,128]{2,1,0:T(8,128)} %broadcast_in_dim_broadcast_in_dim_broadcast_in_dim.2), calls=%async_computation.8 | async-start | bytes 32768 | tf_op jit(solution)/shard_map/all_to_all | solution.py:29
  284.4 0.7 dynamic-slice_bitcast_fusion.1
  285.1 4.6 %all-to-all-done.8 = f32[4,8,128]{2,1,0:T(8,128)S(1)} async-done(((f32[4,8,128]{2,1,0:T(8,128)}), f32[4,8,128]{2,1,0:T(8,128)S(1)}, u32[]{:S(2)}, u32[]{:S(2)}) %all-to-all-start.8) | async-done | bytes 16416 | tf_op jit(solution)/shard_map/all_to_all | solution.py:29
  (52 shorter events, 4.9 us)
Async XLA Ops:
  0.6 0.7 copy-start
  40.7 65.4 %copy-start.1 = (bf16[1,4,64,640]{3,2,1,0:T(8,128)(2,1)S(1)}, bf16[1,4,64,640]{3,2,1,0:T(8,128)(2,1)}, u32[]{:S(2)}) copy-start(bf16[1,4,64,640]{3,2,1,0:T(8,128)(2,1)} %param.7) | copy-start | bytes 983044
  40.7 73.9 %copy-start.4 = (f32[640]{0:T(1024)S(1)}, f32[640]{0:T(1024)}, u32[]{:S(2)}) copy-start(f32[640]{0:T(1024)} %param.9) | copy-start | bytes 7684
  104.2 37.8 %collective-permute-start = (bf16[16,192,768]{2,1,0:T(8,128)(2,1)}, bf16[16,192,768]{2,1,0:T(8,128)(2,1)}, u32[]{:S(2)}, u32[]{:S(2)}) collective-permute-start(bf16[16,192,768]{2,1,0:T(8,128)(2,1)} %all_to_all.46.own), channel_id=1, source_target_pairs={{0,8},{8,0},{1,9},{9,1},{2,10},{10,2},{3,11},{11,3},{4,12},{12,4},... | collective-permute-start | bytes 14155784 | tf_op jit(solution)/shard_map/ppermute | solution.py:69
  106.2 13.8 %collective-permute-start.1 = (bf16[1,64,640]{2,1,0:T(8,128)(2,1)S(1)}, bf16[1,64,640]{2,1,0:T(8,128)(2,1)S(1)}, u32[]{:S(2)}, u32[]{:S(2)}) collective-permute-start(bf16[1,64,640]{2,1,0:T(8,128)(2,1)S(1)} %get-tuple-element.21), channel_id=1, source_target_pairs={{0,1},{1,2},{2,3},{3,4},{4,5},{5,6},{6,7},{8,9},{9,10},{10,11},{11... | collective-permute-start | bytes 245768 | tf_op jit(solution)/shard_map/ppermute | solution.py:41
  113.3 23.5 %collective-permute-start.2 = (bf16[1,64,640]{2,1,0:T(8,128)(2,1)S(1)}, bf16[1,64,640]{2,1,0:T(8,128)(2,1)S(1)}, u32[]{:S(2)}, u32[]{:S(2)}) collective-permute-start(bf16[1,64,640]{2,1,0:T(8,128)(2,1)S(1)} %get-tuple-element.20), channel_id=1, source_target_pairs={{1,0},{2,1},{3,2},{4,3},{5,4},{6,5},{7,6},{9,8},{10,9},{11,10},{12... | collective-permute-start | bytes 245768 | tf_op jit(solution)/shard_map/ppermute | solution.py:41
  120.0 16.7 %copy-start.2 = (bf16[1,64,640]{2,1,0:T(8,128)(2,1)}, bf16[1,64,640]{2,1,0:T(8,128)(2,1)S(1)}, u32[]{:S(2)}) copy-start(bf16[1,64,640]{2,1,0:T(8,128)(2,1)S(1)} %collective-permute-done.1.before) | copy-start | bytes 245764
  136.8 0.6 copy-start.3
  152.0 4.6 %collective-permute-start.3 = (f32[4,64,896]{2,1,0:T(8,128)}, f32[4,64,896]{2,1,0:T(8,128)S(1)}, u32[]{:S(2)}, u32[]{:S(2)}) collective-permute-start(f32[4,64,896]{2,1,0:T(8,128)} %get-tuple-element.12), channel_id=1, source_target_pairs={{0,8},{8,0},{1,9},{9,1},{2,10},{10,2},{3,11},{11,3},{4,12},{12,4},... | collective-permute-start | bytes 2752520 | tf_op jit(solution)/shard_map/ppermute | solution.py:69
  208.5 41.1 %copy-start.5 = (s32[8]{0:T(128)S(1)}, s32[8]{0:T(128)}, u32[]{:S(2)}) copy-start(s32[8]{0:T(128)} %param.13) | copy-start | bytes 100
  245.0 34.6 %all-to-all-start.7 = ((f32[16,8,8,128]{3,2,1,0:T(8,128)}), f32[16,8,8,128]{3,2,1,0:T(8,128)S(1)}, u32[]{:S(2)}, u32[]{:S(2)}) async-start(f32[16,8,8,128]{3,2,1,0:T(8,128)} %broadcast_in_dim.60), calls=%async_computation.7 | async-start | bytes 1048576 | tf_op jit(solution)/shard_map/all_to_all | solution.py:29
  281.2 8.6 %all-to-all-start.8 = ((f32[4,8,128]{2,1,0:T(8,128)}), f32[4,8,128]{2,1,0:T(8,128)S(1)}, u32[]{:S(2)}, u32[]{:S(2)}) async-start(f32[4,8,128]{2,1,0:T(8,128)} %broadcast_in_dim_broadcast_in_dim_broadcast_in_dim.2), calls=%async_computation.8 | async-start | bytes 32768 | tf_op jit(solution)/shard_map/all_to_all | solution.py:29

commit v3 on v2

--- a/solution.py
+++ b/solution.py
@@ -7,6 +7,7 @@
 from jax.experimental.pallas import tpu as pltpu
 from jax.sharding import Mesh
 from jax.sharding import PartitionSpec as P
+
 
 DAMPING = 0.1
 SPLIT = (("zl", 8), ("y", 4), ("c", 2), ("x", 4), ("zh", 2))
@@ -50,15 +51,15 @@
     rows = lax.dynamic_update_slice(rows, outer, (COLS, ROWS))
     got = gather(rows, Z).reshape(2, 8, COLS + 8, 128)
 
-    def merged(part, width):
+    def merged(part):
         flat = part.transpose(0, 2, 1, 3).reshape(part.shape[0] * part.shape[2], -1)
         return jnp.pad(flat, ((0, 0), (0, WIDE - flat.shape[1])))
 
     joined = jnp.concatenate(
         [
-            merged(got[:, :, :COLS, :ROWS], ROWS),
-            merged(got[:, :, COLS:, :ROWS], ROWS),
-            merged(got[:, :, COLS:, ROWS : ROWS + 10], 10),
+            merged(got[:, :, :COLS, :ROWS]),
+            merged(got[:, :, COLS:, :ROWS]),
+            merged(got[:, :, COLS:, ROWS : ROWS + 10]),
         ],
         axis=0,
     )
@@ -190,18 +191,20 @@
     )(core, own, other, patches, bias, cot)
 
 
-def second_kernel(full, patches, grad, partial, scale_in, scale_out):
+def second_kernel(core, own, other, patches, grad, partial, scale_in, scale_out):
     raw_in = jnp.zeros((RANK, 256), F32)
     raw_out = jnp.zeros((RANK, 256), F32)
     square_in = jnp.zeros((RANK, 1), F32)
     square_out = jnp.zeros((RANK, 1), F32)
-    for j in range(8):
-        block = full[j, :, :WIDE]
-        raw_in += dot_last(block, patches[j // 4, j % 4])
-        square_in += jnp.sum(jnp.square(block.astype(F32)), axis=1, keepdims=True)
-        if j < 5:
-            chunk = full[j, :, WIDE:]
-            raw_out += dot_last(chunk, grad[:, j * 128 : j * 128 + 128])
+    me = core[0]
+    for c, half in ((me, own), (1 - me, other)):
+        for y in range(4):
+            block = half[y, :, :WIDE]
+            raw_in += dot_last(block, patches[c, y])
+            square_in += jnp.sum(jnp.square(block.astype(F32)), axis=1, keepdims=True)
+            chunk = half[y, :, WIDE:]
+            lane = pl.multiple_of(jnp.minimum(c * 4 + y, 4) * 128, 128)
+            raw_out += dot_last(chunk, grad[:, pl.ds(lane, 128)])
             square_out += jnp.sum(jnp.square(chunk.astype(F32)), axis=1, keepdims=True)
     root_in, root_out = jnp.sqrt(square_in), jnp.sqrt(square_out)
     feat_in = (raw_in / root_in).astype(BF16)
@@ -211,7 +214,7 @@
     scale_out[...] = root_out
 
 
-def second_pass(full, patches, grad):
+def second_pass(core, own, other, patches, grad):
     return pl.pallas_call(
         second_kernel,
         out_shape=[
@@ -219,9 +222,9 @@
             jax.ShapeDtypeStruct((RANK, 1), F32),
             jax.ShapeDtypeStruct((RANK, 1), F32),
         ],
-        in_specs=[vmem()] * 3,
+        in_specs=[pl.BlockSpec(memory_space=pltpu.SMEM)] + [vmem()] * 4,
         out_specs=[vmem()] * 3,
-    )(full, patches, grad)
+    )(core, own, other, patches, grad)
 
 
 def reduced(kept, sent):
@@ -232,7 +235,7 @@
 
 def spread(part):
     part = gather(part, Z).reshape(16, SLOT)
-    return gather(part, ("c", "y", "x")).reshape(8, RANK, SLOT)
+    return gather(part, ("y", "x")).reshape(4, RANK, SLOT)
 
 
 def per_device(acts, conv_weight, conv_bias, out_cotangent, basis_in, basis_out, query_ids):
@@ -244,25 +247,24 @@
         core, own, swap(own), patches, conv_bias.reshape(1, CH), out_cotangent.reshape(256, CH)
     )
     activated = activated.reshape(acts.shape)
-    full = spread((reduced(kept, sent) / 131072.0).astype(BF16))
-    partial, scale_in, scale_out = second_pass(full, patches, grad_pre)
-
+    fresh = spread((reduced(kept, sent) / 131072.0).astype(BF16))
     zl, y, c, x = (lax.axis_index(a) for a in ("zl", "y", "c", "x"))
-    quarter = partial.reshape(4, 8, 128)
-    sent = jnp.broadcast_to(quarter[None], (8, 4, 8, 128)).reshape(32, 8, 128)
-    got = exchange(lax.optimization_barrier(sent), ("y", "c", "x"))
-    near = got.reshape(8, 4, 8, 128).sum(1)
-    every = gather(near, Z).reshape(2, 8, 8, 8, 128).sum(0).reshape(64, 8, 128)
-    mine = lax.dynamic_index_in_dim(every, lax.axis_index(BATCH), axis=0, keepdims=False)
-    scale = scale_out * scale_in.T + DAMPING
-    scale = lax.dynamic_slice_in_dim(scale, x * 16, 16, axis=0).reshape(8, 128)
-    queries = jnp.take(every, query_ids, axis=0)
-    scores = jnp.sum(queries * (mine / scale)[None], axis=(1, 2)) / (RANK * math.sqrt(RANK))
-    scores = jnp.broadcast_to(scores[:, None], (8, 128))
-    scores = gather(scores, ("x",)).reshape(4, 8, 128).sum(0)[:, :1]
-
-    row = lax.dynamic_index_in_dim(full, c * 4 + y, axis=0, keepdims=False)
+    row = lax.dynamic_index_in_dim(fresh, y, axis=0, keepdims=False)
     basis_in_new = lax.dynamic_slice_in_dim(row[:, : 8 * ROWS], zl * ROWS, ROWS, axis=1).T
+    partial, scale_in, scale_out = second_pass(core, fresh, swap(fresh), patches, grad_pre)
+
+    scale = (scale_out * scale_in.T + DAMPING).reshape(32, 128)
+    scale = lax.dynamic_slice_in_dim(scale, (y * 2 + c) * 4 + x, 1, axis=0)
+    got = exchange(partial.reshape(32, 1, 128), ("y", "c", "x"))
+    near = got.reshape(8, 4, 128).sum(1)
+    every = gather(near, Z).reshape(2, 8, 8, 128).sum(0)
+    mine = lax.dynamic_index_in_dim(every, zl, axis=0, keepdims=False) / scale
+    queries = jnp.take(every.reshape(64, 128), query_ids, axis=0)
+    pairs = jnp.sum(mine[:, None, :] * queries[None, :, :], axis=2)
+    pairs = jnp.pad(pairs / (RANK * math.sqrt(RANK)), ((0, 0), (0, 120)))
+    pairs = jnp.broadcast_to(pairs[:, None, None, :], (8, 4, 1, 128)).reshape(32, 1, 128)
+    scores = exchange(lax.optimization_barrier(pairs), ("y", "c", "x")).sum(0)
+    scores = scores[:, :8].T
     return (activated, basis_in_new, scores)
 
 

time: 291 us -> 276 us (0.948)
  the two profiles are of different devices: /device:TPU:32 before, /device:TPU:1 now
where the time goes in v3:
time: 276 us; the launch traced here: 275 us
  blocking collectives  155 us (56%)
  starting transfers between devices  45.5 us (16%)
  waiting for transfers between devices  39.1 us (14%)
  Pallas kernels  18.7 us (7%)
  local copies, waits for them, and re-layouts  11 us (4%)
  other arithmetic  4.12 us (1%)
    all_to_all x6, blocking collectives, exchange(): return lax.all_to_all(value, axes, 0, 0, tiled=True)  155 us
    all_to_all x3, waiting for transfers between devices, exchange(): return lax.all_to_all(value, axes, 0, 0, tiled=True)  21.9 us
    ppermute x3, starting transfers between devices, swap(): return lax.ppermute(value, 'c', [(0, 1), (1, 0)])  19.4 us
    ppermute x1, waiting for transfers between devices, halo(): lax.ppermute(value[:1], SPACE, down)  13.5 us
    all_to_all x3, starting transfers between devices, exchange(): return lax.all_to_all(value, axes, 0, 0, tiled=True)  12.7 us
    ppermute x1, starting transfers between devices, halo(): lax.ppermute(value[-1:], SPACE, up)  12.2 us
    pallas_call x1, Pallas kernels, first_pass(): pl.pallas_call(first_kernel, grid_spec=pltpu.PrefetchScalarGridSpec(num_s...  9.97 us
  transfers between devices with their start and end apart: 8, of which 6 were waited for; matrix products, arithmetic and copies ran while one was open for 2% of the time, Pallas kernels for 2%

profile of v3, /device:TPU:1, one launch (start us, length us, event | category | flops | bytes accessed | tf_op | source)
XLA Modules:
  0.0 274.6 jit_solution(15544144127094641981)
XLA Ops:
  0.7 0.7 copy-done
  1.4 0.8 dynamic-slice_bitcast_fusion.2
  2.2 0.7 fusion.8
  3.5 31.9 %all_to_all.45 = bf16[16,88,128]{2,1,0:T(8,128)(2,1)S(1)} all-to-all(bf16[16,88,128]{2,1,0:T(8,128)(2,1)S(1)} %broadcast_in_dim.28), channel_id=1, replica_groups=mesh['zl'=8,'y'=4,'c'=2,'x'=4,'zh'=2] {'zh','zl'}, dimensions={0} | all-to-all | bytes 720896 | tf_op jit(solution)/shard_map/all_to_all | solution.py:30
  36.6 56.4 %all_to_all.46.own = bf16[16,192,768]{2,1,0:T(8,128)(2,1)} all-to-all(bf16[16,192,768]{2,1,0:T(8,128)(2,1)S(1)} %broadcast_in_dim.29), channel_id=1, replica_groups=mesh['zl'=8,'y'=4,'c'=2,'x'=4,'zh'=2] {'y','x'}, dimensions={0} | all-to-all | bytes 9437184 | tf_op jit(solution)/shard_map/all_to_all | solution.py:30
  93.0 9.9 %collective-permute-start = (bf16[16,192,768]{2,1,0:T(8,128)(2,1)}, bf16[16,192,768]{2,1,0:T(8,128)(2,1)}, u32[]{:S(2)}, u32[]{:S(2)}) collective-permute-start(bf16[16,192,768]{2,1,0:T(8,128)(2,1)} %all_to_all.46.own), channel_id=1, source_target_pairs={{0,8},{8,0},{1,9},{9,1},{2,10},{10,2},{3,11},{11,3},{4,12},{12,4},... | collective-permute-start | bytes 14155784 | tf_op jit(solution)/shard_map/ppermute | solution.py:70
  102.9 12.2 %collective-permute-start.1 = (bf16[1,64,640]{2,1,0:T(8,128)(2,1)S(1)}, bf16[1,64,640]{2,1,0:T(8,128)(2,1)S(1)}, u32[]{:S(2)}, u32[]{:S(2)}) collective-permute-start(bf16[1,64,640]{2,1,0:T(8,128)(2,1)S(1)} %get-tuple-element.18), channel_id=1, source_target_pairs={{0,1},{1,2},{2,3},{3,4},{4,5},{5,6},{6,7},{8,9},{9,10},{10,11},{11... | collective-permute-start | bytes 245768 | tf_op jit(solution)/shard_map/ppermute | solution.py:42
  115.1 1.3 collective-permute-start.2
  117.0 13.5 %collective-permute-done.2.after = bf16[1,64,640]{2,1,0:T(8,128)(2,1)S(1)} collective-permute-done((bf16[1,64,640]{2,1,0:T(8,128)(2,1)S(1)}, bf16[1,64,640]{2,1,0:T(8,128)(2,1)S(1)}, u32[]{:S(2)}, u32[]{:S(2)}) %collective-permute-start.2) | collective-permute-done | bytes 81952 | tf_op jit(solution)/shard_map/ppermute | solution.py:42
  131.2 4.6 %shard_map.94.patches = bf16[2,4,256,768]{3,2,1,0:T(8,128)(2,1)} custom-call(bf16[1,64,640]{2,1,0:T(8,128)(2,1)} %copy-done.4, bf16[4,64,640]{2,1,0:T(8,128)(2,1)} %bitcast.55, bf16[1,64,640]{2,1,0:T(8,128)(2,1)} %copy-done.5), custom_call_target="tpu_custom_call" | custom-call | tf_op jit(solution)/shard_map/pallas_call | solution.py:107
  135.8 10.0 %shard_map.95 = (bf16[256,640]{1,0:T(8,128)(2,1)}, bf16[256,640]{1,0:T(8,128)(2,1)}, f32[4,64,896]{2,1,0:T(8,128)}, f32[4,64,896]{2,1,0:T(8,128)}) custom-call(s32[1]{0:T(128)} %bitcast.core, bf16[16,192,768]{2,1,0:T(8,128)(2,1)} %all_to_all.46.own, bf16[16,192,768]{2,1,0:T(8,128)(2,1)} %collective-permute-done.other, ...), custom_call_target="tpu_custom_call" | custom-call | tf_op jit(solution)/shard_map/pallas_call | solution.py:167
  145.8 2.6 collective-permute-start.3
  148.5 2.3 collective-permute-done.3
  150.7 1.3 add.53
  152.0 21.4 %all_to_all.47 = f32[16,16,896]{2,1,0:T(8,128)S(1)} all-to-all(f32[16,16,896]{2,1,0:T(8,128)S(1)} %bitcast.48), channel_id=1, replica_groups=mesh['zl'=8,'y'=4,'c'=2,'x'=4,'zh'=2] {'y','x'}, dimensions={0} | all-to-all | bytes 1835008 | tf_op jit(solution)/shard_map/all_to_all | solution.py:30
  173.5 19.3 %all_to_all.48 = f32[16,7,128]{2,1,0:T(8,128)S(1)} all-to-all(f32[16,7,128]{2,1,0:T(8,128)S(1)} %reshape.124), channel_id=1, replica_groups=mesh['zl'=8,'y'=4,'c'=2,'x'=4,'zh'=2] {'zh','zl'}, dimensions={0} | all-to-all | bytes 114688 | tf_op jit(solution)/shard_map/all_to_all | solution.py:30
  192.8 14.3 %all_to_all.49 = bf16[16,7,128]{2,1,0:T(8,128)(2,1)S(1)} all-to-all(bf16[16,7,128]{2,1,0:T(8,128)(2,1)S(1)} %broadcast_in_dim.30), channel_id=1, replica_groups=mesh['zl'=8,'y'=4,'c'=2,'x'=4,'zh'=2] {'zh','zl'}, dimensions={0} | all-to-all | bytes 57344 | tf_op jit(solution)/shard_map/all_to_all | solution.py:30
  207.2 11.8 %all_to_all.50 = bf16[16,16,896]{2,1,0:T(8,128)(2,1)S(1)} all-to-all(bf16[16,16,896]{2,1,0:T(8,128)(2,1)S(1)} %broadcast_in_dim.57), channel_id=1, replica_groups=mesh['zl'=8,'y'=4,'c'=2,'x'=4,'zh'=2] {'y','x'}, dimensions={0} | all-to-all | bytes 917504 | tf_op jit(solution)/shard_map/all_to_all | solution.py:30
  219.0 6.8 %collective-permute-start.4 = (bf16[4,64,896]{2,1,0:T(8,128)(2,1)S(1)}, bf16[4,64,896]{2,1,0:T(8,128)(2,1)S(1)}, u32[]{:S(2)}, u32[]{:S(2)}) collective-permute-start(bf16[4,64,896]{2,1,0:T(8,128)(2,1)S(1)} %bitcast.49), channel_id=1, source_target_pairs={{0,8},{8,0},{1,9},{9,1},{2,10},{10,2},{3,11},{11,3},{4,12},{12,4},... | collective-permute-start | bytes 1376264 | tf_op jit(solution)/shard_map/ppermute | solution.py:70
  225.9 1.4 collective-permute-done.4.other
  227.3 0.8 copy-done.3
  228.0 4.1 %shard_map.96 = (f32[64,64]{1,0:T(8,128)}, f32[64,1]{1,0:T(8,128)}, f32[64,1]{1,0:T(8,128)}) custom-call(s32[1]{0:T(128)} %bitcast.core, bf16[4,64,896]{2,1,0:T(8,128)(2,1)} %bitcast.50, bf16[4,64,896]{2,1,0:T(8,128)(2,1)} %copy-done.3, bf16[2,4,256,768]{3,2,1,0:T(8,128)(2,1)} %shard_map.94.patches, bf16[256,640]{1,0:T(8,128)(2,1)} %get-tuple-element.13.grad), custom_call_target="tpu_custom_call" | custom-call | tf_op jit(solution)/shard_map/pallas_call | solution.py:218
  232.2 1.4 reshape.126
  233.6 3.9 %all-to-all-start.6 = ((f32[32,1,128]{2,1,0:T(1,128)}), f32[32,1,128]{2,1,0:T(1,128)S(1)}, u32[]{:S(2)}, u32[]{:S(2)}) async-start(f32[32,1,128]{2,1,0:T(1,128)} %bitcast.17), calls=%async_computation.6 | async-start | bytes 32768 | tf_op jit(solution)/shard_map/all_to_all | solution.py:30
  237.5 6.9 %all-to-all-done.6 = f32[32,1,128]{2,1,0:T(1,128)S(1)} async-done(((f32[32,1,128]{2,1,0:T(1,128)}), f32[32,1,128]{2,1,0:T(1,128)S(1)}, u32[]{:S(2)}, u32[]{:S(2)}) %all-to-all-start.6) | async-done | bytes 16416 | tf_op jit(solution)/shard_map/all_to_all | solution.py:30
  245.1 3.5 %all-to-all-start.7 = ((f32[16,8,128]{2,1,0:T(8,128)}), f32[16,8,128]{2,1,0:T(8,128)S(1)}, u32[]{:S(2)}, u32[]{:S(2)}) async-start(f32[16,8,128]{2,1,0:T(8,128)} %broadcast_in_dim.58), calls=%async_computation.7 | async-start | bytes 131072 | tf_op jit(solution)/shard_map/all_to_all | solution.py:30
  248.6 0.9 dynamic-slice_bitcast_fusion
  249.5 0.9 reduce.1
  250.7 0.9 reduce.2
  251.7 8.7 %all-to-all-done.7 = f32[16,8,128]{2,1,0:T(8,128)S(1)} async-done(((f32[16,8,128]{2,1,0:T(8,128)}), f32[16,8,128]{2,1,0:T(8,128)S(1)}, u32[]{:S(2)}, u32[]{:S(2)}) %all-to-all-start.7) | async-done | bytes 65568 | tf_op jit(solution)/shard_map/all_to_all | solution.py:30
  261.7 5.3 %all-to-all-start.8 = ((f32[32,1,128]{2,1,0:T(1,128)}), f32[32,1,128]{2,1,0:T(1,128)S(1)}, u32[]{:S(2)}, u32[]{:S(2)}) async-start(f32[32,1,128]{2,1,0:T(1,128)} %bitcast.23), calls=%async_computation.8 | async-start | bytes 32768 | tf_op jit(solution)/shard_map/all_to_all | solution.py:30
  267.7 6.3 %all-to-all-done.8 = f32[32,1,128]{2,1,0:T(1,128)S(1)} async-done(((f32[32,1,128]{2,1,0:T(1,128)}), f32[32,1,128]{2,1,0:T(1,128)S(1)}, u32[]{:S(2)}, u32[]{:S(2)}) %all-to-all-start.8) | async-done | bytes 16416 | tf_op jit(solution)/shard_map/all_to_all | solution.py:30
  (62 shorter events, 6.8 us)
Async XLA Ops:
  0.6 0.7 copy-start
  36.6 66.3 %copy-start.2 = (bf16[1,4,64,640]{3,2,1,0:T(8,128)(2,1)S(1)}, bf16[1,4,64,640]{3,2,1,0:T(8,128)(2,1)}, u32[]{:S(2)}) copy-start(bf16[1,4,64,640]{3,2,1,0:T(8,128)(2,1)} %param.7) | copy-start | bytes 983044
  36.6 79.8 %copy-start.6 = (f32[640]{0:T(1024)S(1)}, f32[640]{0:T(1024)}, u32[]{:S(2)}) copy-start(f32[640]{0:T(1024)} %param.9) | copy-start | bytes 7684
  93.0 42.9 %collective-permute-start = (bf16[16,192,768]{2,1,0:T(8,128)(2,1)}, bf16[16,192,768]{2,1,0:T(8,128)(2,1)}, u32[]{:S(2)}, u32[]{:S(2)}) collective-permute-start(bf16[16,192,768]{2,1,0:T(8,128)(2,1)} %all_to_all.46.own), channel_id=1, source_target_pairs={{0,8},{8,0},{1,9},{9,1},{2,10},{10,2},{3,11},{11,3},{4,12},{12,4},... | collective-permute-start | bytes 14155784 | tf_op jit(solution)/shard_map/ppermute | solution.py:70
  102.9 14.1 %collective-permute-start.1 = (bf16[1,64,640]{2,1,0:T(8,128)(2,1)S(1)}, bf16[1,64,640]{2,1,0:T(8,128)(2,1)S(1)}, u32[]{:S(2)}, u32[]{:S(2)}) collective-permute-start(bf16[1,64,640]{2,1,0:T(8,128)(2,1)S(1)} %get-tuple-element.18), channel_id=1, source_target_pairs={{0,1},{1,2},{2,3},{3,4},{4,5},{5,6},{6,7},{8,9},{9,10},{10,11},{11... | collective-permute-start | bytes 245768 | tf_op jit(solution)/shard_map/ppermute | solution.py:42
  115.1 15.4 %collective-permute-start.2 = (bf16[1,64,640]{2,1,0:T(8,128)(2,1)S(1)}, bf16[1,64,640]{2,1,0:T(8,128)(2,1)S(1)}, u32[]{:S(2)}, u32[]{:S(2)}) collective-permute-start(bf16[1,64,640]{2,1,0:T(8,128)(2,1)S(1)} %get-tuple-element.17), channel_id=1, source_target_pairs={{1,0},{2,1},{3,2},{4,3},{5,4},{6,5},{7,6},{9,8},{10,9},{11,10},{12... | collective-permute-start | bytes 245768 | tf_op jit(solution)/shard_map/ppermute | solution.py:42
  117.0 13.5 %copy-start.4 = (bf16[1,64,640]{2,1,0:T(8,128)(2,1)}, bf16[1,64,640]{2,1,0:T(8,128)(2,1)S(1)}, u32[]{:S(2)}) copy-start(bf16[1,64,640]{2,1,0:T(8,128)(2,1)S(1)} %collective-permute-done.1.before) | copy-start | bytes 245764
  130.6 0.6 copy-start.5
  145.8 80.0 %copy-start.7 = (s32[8]{0:T(128)S(1)}, s32[8]{0:T(128)}, u32[]{:S(2)}) copy-start(s32[8]{0:T(128)} %param.13) | copy-start | bytes 100
  145.8 4.9 %collective-permute-start.3 = (f32[4,64,896]{2,1,0:T(8,128)}, f32[4,64,896]{2,1,0:T(8,128)S(1)}, u32[]{:S(2)}, u32[]{:S(2)}) collective-permute-start(f32[4,64,896]{2,1,0:T(8,128)} %get-tuple-element.12), channel_id=1, source_target_pairs={{0,8},{8,0},{1,9},{9,1},{2,10},{10,2},{3,11},{11,3},{4,12},{12,4},... | collective-permute-start | bytes 2752520 | tf_op jit(solution)/shard_map/ppermute | solution.py:70
  219.0 8.3 %copy-start.1 = (bf16[16,16,896]{2,1,0:T(8,128)(2,1)}, bf16[16,16,896]{2,1,0:T(8,128)(2,1)S(1)}, u32[]{:S(2)}) copy-start(bf16[16,16,896]{2,1,0:T(8,128)(2,1)S(1)} %all_to_all.50) | copy-start | bytes 1376260
  219.0 8.3 %collective-permute-start.4 = (bf16[4,64,896]{2,1,0:T(8,128)(2,1)S(1)}, bf16[4,64,896]{2,1,0:T(8,128)(2,1)S(1)}, u32[]{:S(2)}, u32[]{:S(2)}) collective-permute-start(bf16[4,64,896]{2,1,0:T(8,128)(2,1)S(1)} %bitcast.49), channel_id=1, source_target_pairs={{0,8},{8,0},{1,9},{9,1},{2,10},{10,2},{3,11},{11,3},{4,12},{12,4},... | collective-permute-start | bytes 1376264 | tf_op jit(solution)/shard_map/ppermute | solution.py:70
  227.3 0.8 copy-start.3
  233.6 10.9 %all-to-all-start.6 = ((f32[32,1,128]{2,1,0:T(1,128)}), f32[32,1,128]{2,1,0:T(1,128)S(1)}, u32[]{:S(2)}, u32[]{:S(2)}) async-start(f32[32,1,128]{2,1,0:T(1,128)} %bitcast.17), calls=%async_computation.6 | async-start | bytes 32768 | tf_op jit(solution)/shard_map/all_to_all | solution.py:30
  245.1 15.2 %all-to-all-start.7 = ((f32[16,8,128]{2,1,0:T(8,128)}), f32[16,8,128]{2,1,0:T(8,128)S(1)}, u32[]{:S(2)}, u32[]{:S(2)}) async-start(f32[16,8,128]{2,1,0:T(8,128)} %broadcast_in_dim.58), calls=%async_computation.7 | async-start | bytes 131072 | tf_op jit(solution)/shard_map/all_to_all | solution.py:30
  261.7 12.4 %all-to-all-start.8 = ((f32[32,1,128]{2,1,0:T(1,128)}), f32[32,1,128]{2,1,0:T(1,128)S(1)}, u32[]{:S(2)}, u32[]{:S(2)}) async-start(f32[32,1,128]{2,1,0:T(1,128)} %bitcast.23), calls=%async_computation.8 | async-start | bytes 32768 | tf_op jit(solution)/shard_map/all_to_all | solution.py:30
